TPU v7x, 32 devices: a whole 2x2x4 slice. The times are simulated.
32 devices in a mesh: rep: 4 (over y, core), shard: 8 (over z, x).
Axes of the slice: x: 2, y: 2, z: 4, core: 2. Of those that a mesh axis runs over, the one named last changes fastest.
Arguments:
- hidden: bfloat16 [6144, 1280], P(('rep', 'shard')), may hold values from -6 to 6
- out_grad: bfloat16 [6144, 1280], P(('rep', 'shard')), may hold values from -6 to 6
- clip_lengths: int32 [4], P('rep'), may hold values from 768 to 1536, as said below
- adapter_index: int32 [4], P('rep'), may hold values from 0 to 7
- w_query: bfloat16 [1280, 1280], P('shard'), may hold values from -0.15625 to 0.15625
- w_key: bfloat16 [1280, 1280], P('shard'), may hold values from -0.15625 to 0.15625
- w_value: bfloat16 [1280, 1280], P('shard'), may hold values from -0.15625 to 0.15625
- w_output: bfloat16 [1280, 1280], P('shard'), may hold values from -3 to 3
- w_up: bfloat16 [1280, 5120], P('shard'), may hold values from -0.15625 to 0.15625
- w_down: bfloat16 [5120, 1280], P('shard'), may hold values from -0.078125 to 0.078125
- a_query: bfloat16 [8, 1280, 16], P(None, 'shard'), may hold values from -0.15625 to 0.15625
- b_query: bfloat16 [8, 16, 1280], P(None, None, 'shard'), may hold values from -0.75 to 0.75
- a_key: bfloat16 [8, 1280, 16], P(None, 'shard'), may hold values from -0.15625 to 0.15625
- b_key: bfloat16 [8, 16, 1280], P(None, None, 'shard'), may hold values from -0.75 to 0.75
- a_value: bfloat16 [8, 1280, 16], P(None, 'shard'), may hold values from -0.15625 to 0.15625
- b_value: bfloat16 [8, 16, 1280], P(None, None, 'shard'), may hold values from -0.75 to 0.75
- a_output: bfloat16 [8, 1280, 16], P(None, 'shard'), may hold values from -3 to 3
- b_output: bfloat16 [8, 16, 1280], P(None, None, 'shard'), may hold values from -0.75 to 0.75
- a_up: bfloat16 [8, 1280, 16], P(None, 'shard'), may hold values from -0.15625 to 0.15625
- b_up: bfloat16 [8, 16, 5120], P(None, None, 'shard'), may hold values from -0.75 to 0.75
- a_down: bfloat16 [8, 5120, 16], P(None, 'shard'), may hold values from -0.078125 to 0.078125
- b_down: bfloat16 [8, 16, 1280], P(None, None, 'shard'), may hold values from -0.75 to 0.75
Outputs:
- layer_out: bfloat16 [6144, 1280], P(('rep', 'shard'))
- input_grad: bfloat16 [6144, 1280], P(('rep', 'shard'))
- grad_a_query: float32 [8, 1280, 16], P(None, 'shard')
- grad_b_query: float32 [8, 16, 1280], P(None, None, 'shard')
- grad_a_key: float32 [8, 1280, 16], P(None, 'shard')
- grad_b_key: float32 [8, 16, 1280], P(None, None, 'shard')
- grad_a_value: float32 [8, 1280, 16], P(None, 'shard')
- grad_b_value: float32 [8, 16, 1280], P(None, None, 'shard')
- grad_a_output: float32 [8, 1280, 16], P(None, 'shard')
- grad_b_output: float32 [8, 16, 1280], P(None, None, 'shard')
- grad_a_up: float32 [8, 1280, 16], P(None, 'shard')
- grad_b_up: float32 [8, 16, 5120], P(None, None, 'shard')
- grad_a_down: float32 [8, 5120, 16], P(None, 'shard')
- grad_b_down: float32 [8, 16, 1280], P(None, None, 'shard')
Inputs may be any that keep to these rules, and one draw needn't show every extreme that they name: `clip_lengths`: slots of a clip at positions of its length or more are padding; some clip has length exactly 1536.
All inputs are finite; a program needn't handle non-finite values.
Results may differ from a plain program's by a relative error of at most 0.02.
Values may be sent and summed in bfloat16 or wider, within the bound.
No kernel may reach another device: no remote copies, remote signals or barrier semaphores. Data moves between devices by JAX's collectives and lax.ppermute only.
A program may use at most 256 MiB of HBM per device.

v0:
```python
from functools import partial

import jax
import jax.numpy as jnp
from jax import lax
from jax.sharding import PartitionSpec as P

D = 1280
HEADS = 16
HEAD = 80


EPSILON = 1e-05
NEGATIVE = -1e30


def normalize(values):
    center = values - jnp.mean(values, axis=-1, keepdims=True)
    spread = jnp.mean(center * center, axis=-1, keepdims=True)
    return center * lax.rsqrt(spread + EPSILON)


def adapted(inputs, weight, enter, leave):
    inner = jnp.dot(inputs, enter, preferred_element_type=jnp.float32).astype(jnp.bfloat16)
    result = jnp.dot(inputs, weight, preferred_element_type=jnp.float32)
    return (result + jnp.dot(inner, leave, preferred_element_type=jnp.float32), inner)


def adapted_back(inputs, inner, grad_out, weight, enter, leave):
    grad_leave = jnp.einsum("tr,to->ro", inner, grad_out, preferred_element_type=jnp.float32)
    grad_inner = jnp.einsum(
        "to,ro->tr", grad_out, leave, preferred_element_type=jnp.float32
    ).astype(jnp.bfloat16)
    grad_enter = jnp.einsum("ti,tr->ir", inputs, grad_inner, preferred_element_type=jnp.float32)
    grad_inputs = jnp.einsum("to,io->ti", grad_out, weight, preferred_element_type=jnp.float32)
    grad_inputs = grad_inputs + jnp.einsum(
        "tr,ir->ti", grad_inner, enter, preferred_element_type=jnp.float32
    )
    return (grad_inputs, grad_enter, grad_leave)


def attend(queries, keys, values, key_valid, score_scale):
    head_total = queries.shape[1]
    group_size = 4

    def attend_group_step(step_index, carried):
        context, log_totals = carried
        offset = step_index * group_size
        query_group = lax.dynamic_slice_in_dim(queries, offset, group_size, 1)
        key_group = lax.dynamic_slice_in_dim(keys, offset, group_size, 1)
        value_group = lax.dynamic_slice_in_dim(values, offset, group_size, 1)
        scores = (
            jnp.einsum("qhe,khe->hqk", query_group, key_group, preferred_element_type=jnp.float32)
            * score_scale
        )
        scores = jnp.where(key_valid[None, None, :], scores, NEGATIVE)
        highest = jnp.max(scores, axis=2, keepdims=True)
        shifted = jnp.exp(scores - highest)
        totals = jnp.sum(shifted, axis=2, keepdims=True)
        weights = (shifted / totals).astype(jnp.bfloat16)
        portion = jnp.einsum(
            "hqk,khe->qhe", weights, value_group, preferred_element_type=jnp.float32
        )
        context = lax.dynamic_update_slice_in_dim(context, portion, offset, 1)
        log_part = jnp.transpose((highest + jnp.log(totals))[:, :, 0])
        log_totals = lax.dynamic_update_slice_in_dim(log_totals, log_part, offset, 1)
        return (context, log_totals)

    initial = (
        jnp.zeros(queries.shape, jnp.float32),
        jnp.zeros((queries.shape[0], head_total), jnp.float32),
    )
    return lax.fori_loop(0, head_total // group_size, attend_group_step, initial)


def attention_back(
    queries,
    grad_context,
    log_totals,
    given_delta,
    keys,
    values,
    key_valid,
    score_scale,
    want_queries,
    want_keys,
):
    head_total = queries.shape[1]
    group_size = 4

    def attention_group_step(step_index, carried):
        grad_q, grad_k, grad_v, deltas = carried
        offset = step_index * group_size
        query_group = lax.dynamic_slice_in_dim(queries, offset, group_size, 1)
        dout_group = lax.dynamic_slice_in_dim(grad_context, offset, group_size, 1)
        key_group = lax.dynamic_slice_in_dim(keys, offset, group_size, 1)
        value_group = lax.dynamic_slice_in_dim(values, offset, group_size, 1)
        scores = (
            jnp.einsum("qhe,khe->hqk", query_group, key_group, preferred_element_type=jnp.float32)
            * score_scale
        )
        scores = jnp.where(key_valid[None, None, :], scores, NEGATIVE)
        lse_group = jnp.transpose(lax.dynamic_slice_in_dim(log_totals, offset, group_size, 1))[
            :, :, None
        ]
        weights = jnp.exp(scores - lse_group)
        grad_weights = jnp.einsum(
            "qhe,khe->hqk", dout_group, value_group, preferred_element_type=jnp.float32
        )
        if given_delta is None:
            row_delta = jnp.sum(weights * grad_weights, axis=2)
            deltas = lax.dynamic_update_slice_in_dim(deltas, jnp.transpose(row_delta), offset, 1)
        else:
            row_delta = jnp.transpose(lax.dynamic_slice_in_dim(given_delta, offset, group_size, 1))
        grad_scores = (weights * (grad_weights - row_delta[:, :, None])).astype(jnp.bfloat16)
        if want_queries:
            query_part = jnp.einsum(
                "hqk,khe->qhe", grad_scores, key_group, preferred_element_type=jnp.float32
            )
            grad_q = lax.dynamic_update_slice_in_dim(grad_q, query_part * score_scale, offset, 1)
        if want_keys:
            key_part = jnp.einsum(
                "hqk,qhe->khe", grad_scores, query_group, preferred_element_type=jnp.float32
            )
            grad_k = lax.dynamic_update_slice_in_dim(grad_k, key_part * score_scale, offset, 1)
            value_part = jnp.einsum(
                "hqk,qhe->khe",
                weights.astype(jnp.bfloat16),
                dout_group,
                preferred_element_type=jnp.float32,
            )
            grad_v = lax.dynamic_update_slice_in_dim(grad_v, value_part, offset, 1)
        return (grad_q, grad_k, grad_v, deltas)

    initial = (
        jnp.zeros(queries.shape, jnp.float32) if want_queries else None,
        jnp.zeros(keys.shape, jnp.float32) if want_keys else None,
        jnp.zeros(values.shape, jnp.float32) if want_keys else None,
        jnp.zeros((queries.shape[0], head_total), jnp.float32) if given_delta is None else None,
    )
    return lax.fori_loop(0, head_total // group_size, attention_group_step, initial)


def body(
    hidden,
    out_grad,
    clip_lengths,
    adapter_index,
    w_query,
    w_key,
    w_value,
    w_output,
    w_up,
    w_down,
    a_query,
    b_query,
    a_key,
    b_key,
    a_value,
    b_value,
    a_output,
    b_output,
    a_up,
    b_up,
    a_down,
    b_down,
):
    tok_rows = hidden.shape[0]
    shards = lax.axis_size("shard")
    seq_len = tok_rows * shards
    length = clip_lengths[0]
    chosen = adapter_index[0]
    score_scale = HEAD ** (-0.5)

    def pick_set(tables):
        return lax.dynamic_index_in_dim(tables, chosen, 0, keepdims=False)

    enter_q, leave_q = (pick_set(a_query), pick_set(b_query))
    enter_k, leave_k = (pick_set(a_key), pick_set(b_key))
    enter_v, leave_v = (pick_set(a_value), pick_set(b_value))
    enter_o, leave_o = (pick_set(a_output), pick_set(b_output))
    enter_u, leave_u = (pick_set(a_up), pick_set(b_up))
    enter_d, leave_d = (pick_set(a_down), pick_set(b_down))
    attn_full = (
        lax.all_gather(w_query, "shard", axis=0, tiled=True),
        lax.all_gather(w_key, "shard", axis=0, tiled=True),
        lax.all_gather(w_value, "shard", axis=0, tiled=True),
        lax.all_gather(w_output, "shard", axis=0, tiled=True),
        lax.all_gather(enter_q, "shard", axis=0, tiled=True),
        lax.all_gather(leave_q, "shard", axis=1, tiled=True),
        lax.all_gather(enter_k, "shard", axis=0, tiled=True),
        lax.all_gather(leave_k, "shard", axis=1, tiled=True),
        lax.all_gather(enter_v, "shard", axis=0, tiled=True),
        lax.all_gather(leave_v, "shard", axis=1, tiled=True),
        lax.all_gather(enter_o, "shard", axis=0, tiled=True),
        lax.all_gather(leave_o, "shard", axis=1, tiled=True),
    )
    (
        query_weight,
        key_weight,
        value_weight,
        output_weight,
        query_enter,
        query_leave,
        key_enter,
        key_leave,
        value_enter,
        value_leave,
        output_enter,
        output_leave,
    ) = attn_full
    inputs = hidden.astype(jnp.float32)
    first_in = normalize(inputs).astype(jnp.bfloat16)
    query_f, query_inner = adapted(first_in, query_weight, query_enter, query_leave)
    key_f, key_inner = adapted(first_in, key_weight, key_enter, key_leave)
    value_f, value_inner = adapted(first_in, value_weight, value_enter, value_leave)
    query_b = query_f.astype(jnp.bfloat16)
    key_b = key_f.astype(jnp.bfloat16)
    value_b = value_f.astype(jnp.bfloat16)
    key_all, value_all = (
        lax.all_gather(key_b, "shard", axis=0, tiled=True),
        lax.all_gather(value_b, "shard", axis=0, tiled=True),
    )
    key_valid = jnp.arange(seq_len) < length
    query_heads = query_b.reshape(tok_rows, HEADS, HEAD)
    key_heads = key_all.reshape(seq_len, HEADS, HEAD)
    value_heads = value_all.reshape(seq_len, HEADS, HEAD)
    attn_heads, row_lse = attend(query_heads, key_heads, value_heads, key_valid, score_scale)
    context = attn_heads.reshape(tok_rows, D).astype(jnp.bfloat16)
    branch, output_inner = adapted(context, output_weight, output_enter, output_leave)
    middle = inputs + branch
    second_in = normalize(middle).astype(jnp.bfloat16)
    mlp_full = (
        lax.all_gather(w_up, "shard", axis=0, tiled=True),
        lax.all_gather(w_down, "shard", axis=0, tiled=True),
        lax.all_gather(enter_u, "shard", axis=0, tiled=True),
        lax.all_gather(leave_u, "shard", axis=1, tiled=True),
        lax.all_gather(enter_d, "shard", axis=0, tiled=True),
        lax.all_gather(leave_d, "shard", axis=1, tiled=True),
    )
    up_weight, down_weight, up_enter, up_leave, down_enter, down_leave = mlp_full
    pre_act, up_inner = adapted(second_in, up_weight, up_enter, up_leave)
    activated = jax.nn.gelu(pre_act, approximate=False).astype(jnp.bfloat16)
    mlp_branch, down_inner = adapted(activated, down_weight, down_enter, down_leave)
    layer_out = (middle + mlp_branch).astype(jnp.bfloat16)
    grad_act, grad_enter_d, grad_leave_d = adapted_back(
        activated, down_inner, out_grad, down_weight, down_enter, down_leave
    )
    unused_gelu, gelu_pull = jax.vjp(partial(jax.nn.gelu, approximate=False), pre_act)
    grad_pre = gelu_pull(grad_act)[0].astype(jnp.bfloat16)
    grad_second, grad_enter_u, grad_leave_u = adapted_back(
        second_in, up_inner, grad_pre, up_weight, up_enter, up_leave
    )
    unused_second, second_pull = jax.vjp(normalize, middle)
    grad_middle = out_grad.astype(jnp.float32) + second_pull(grad_second)[0]
    grad_branch = grad_middle.astype(jnp.bfloat16)
    grad_context, grad_enter_o, grad_leave_o = adapted_back(
        context, output_inner, grad_branch, output_weight, output_enter, output_leave
    )
    grad_context_b = grad_context.astype(jnp.bfloat16)
    grad_context_heads = grad_context_b.reshape(tok_rows, HEADS, HEAD)
    grad_query, unused_k, unused_v, row_delta = attention_back(
        query_heads,
        grad_context_heads,
        row_lse,
        None,
        key_heads,
        value_heads,
        key_valid,
        score_scale,
        True,
        False,
    )
    unused_q, grad_k, grad_v, unused_delta = attention_back(
        query_heads,
        grad_context_heads,
        row_lse,
        row_delta,
        key_heads,
        value_heads,
        key_valid,
        score_scale,
        False,
        True,
    )
    joined = lax.psum_scatter(
        jnp.concatenate(
            (
                grad_k.reshape(tok_rows * lax.axis_size("shard"), D),
                grad_v.reshape(tok_rows * lax.axis_size("shard"), D),
            ),
            axis=1,
        ).astype(jnp.bfloat16),
        "shard",
        scatter_dimension=0,
        tiled=True,
    ).astype(jnp.float32)
    grad_key = joined[:, :D]
    grad_value = joined[:, D:]
    grad_query_b = grad_query.reshape(tok_rows, D).astype(jnp.bfloat16)
    grad_key_b = grad_key.astype(jnp.bfloat16)
    grad_value_b = grad_value.astype(jnp.bfloat16)
    from_query, grad_enter_q, grad_leave_q = adapted_back(
        first_in, query_inner, grad_query_b, query_weight, query_enter, query_leave
    )
    from_key, grad_enter_k, grad_leave_k = adapted_back(
        first_in, key_inner, grad_key_b, key_weight, key_enter, key_leave
    )
    from_value, grad_enter_v, grad_leave_v = adapted_back(
        first_in, value_inner, grad_value_b, value_weight, value_enter, value_leave
    )
    grad_first = from_query + from_key + from_value
    unused_first, first_pull = jax.vjp(normalize, inputs)
    input_grad = (grad_middle + first_pull(grad_first)[0]).astype(jnp.bfloat16)
    owned = (
        lax.psum_scatter(
            grad_enter_q.astype(jnp.bfloat16), "shard", scatter_dimension=0, tiled=True
        ).astype(jnp.float32),
        lax.psum_scatter(
            grad_leave_q.astype(jnp.bfloat16), "shard", scatter_dimension=1, tiled=True
        ).astype(jnp.float32),
        lax.psum_scatter(
            grad_enter_k.astype(jnp.bfloat16), "shard", scatter_dimension=0, tiled=True
        ).astype(jnp.float32),
        lax.psum_scatter(
            grad_leave_k.astype(jnp.bfloat16), "shard", scatter_dimension=1, tiled=True
        ).astype(jnp.float32),
        lax.psum_scatter(
            grad_enter_v.astype(jnp.bfloat16), "shard", scatter_dimension=0, tiled=True
        ).astype(jnp.float32),
        lax.psum_scatter(
            grad_leave_v.astype(jnp.bfloat16), "shard", scatter_dimension=1, tiled=True
        ).astype(jnp.float32),
        lax.psum_scatter(
            grad_enter_o.astype(jnp.bfloat16), "shard", scatter_dimension=0, tiled=True
        ).astype(jnp.float32),
        lax.psum_scatter(
            grad_leave_o.astype(jnp.bfloat16), "shard", scatter_dimension=1, tiled=True
        ).astype(jnp.float32),
        lax.psum_scatter(
            grad_enter_u.astype(jnp.bfloat16), "shard", scatter_dimension=0, tiled=True
        ).astype(jnp.float32),
        lax.psum_scatter(
            grad_leave_u.astype(jnp.bfloat16), "shard", scatter_dimension=1, tiled=True
        ).astype(jnp.float32),
        lax.psum_scatter(
            grad_enter_d.astype(jnp.bfloat16), "shard", scatter_dimension=0, tiled=True
        ).astype(jnp.float32),
        lax.psum_scatter(
            grad_leave_d.astype(jnp.bfloat16), "shard", scatter_dimension=1, tiled=True
        ).astype(jnp.float32),
    )
    selector = (jnp.arange(a_query.shape[0]) == chosen).astype(jnp.float32)
    placed = [selector[:, None, None] * piece[None] for piece in owned]
    totals = (
        lax.psum(placed[0].astype(jnp.bfloat16), "rep").astype(jnp.float32),
        lax.psum(placed[1].astype(jnp.bfloat16), "rep").astype(jnp.float32),
        lax.psum(placed[2].astype(jnp.bfloat16), "rep").astype(jnp.float32),
        lax.psum(placed[3].astype(jnp.bfloat16), "rep").astype(jnp.float32),
        lax.psum(placed[4].astype(jnp.bfloat16), "rep").astype(jnp.float32),
        lax.psum(placed[5].astype(jnp.bfloat16), "rep").astype(jnp.float32),
        lax.psum(placed[6].astype(jnp.bfloat16), "rep").astype(jnp.float32),
        lax.psum(placed[7].astype(jnp.bfloat16), "rep").astype(jnp.float32),
        lax.psum(placed[8].astype(jnp.bfloat16), "rep").astype(jnp.float32),
        lax.psum(placed[9].astype(jnp.bfloat16), "rep").astype(jnp.float32),
        lax.psum(placed[10].astype(jnp.bfloat16), "rep").astype(jnp.float32),
        lax.psum(placed[11].astype(jnp.bfloat16), "rep").astype(jnp.float32),
    )
    return (
        layer_out,
        input_grad,
        totals[0],
        totals[1],
        totals[2],
        totals[3],
        totals[4],
        totals[5],
        totals[6],
        totals[7],
        totals[8],
        totals[9],
        totals[10],
        totals[11],
    )


def solution(mesh):
    return jax.shard_map(
        body,
        mesh=mesh,
        in_specs=(
            P(("rep", "shard"), None),
            P(("rep", "shard"), None),
            P("rep"),
            P("rep"),
            P("shard", None),
            P("shard", None),
            P("shard", None),
            P("shard", None),
            P("shard", None),
            P("shard", None),
            P(None, "shard", None),
            P(None, None, "shard"),
            P(None, "shard", None),
            P(None, None, "shard"),
            P(None, "shard", None),
            P(None, None, "shard"),
            P(None, "shard", None),
            P(None, None, "shard"),
            P(None, "shard", None),
            P(None, None, "shard"),
            P(None, "shard", None),
            P(None, None, "shard"),
        ),
        out_specs=(
            P(("rep", "shard"), None),
            P(("rep", "shard"), None),
            P(None, "shard", None),
            P(None, None, "shard"),
            P(None, "shard", None),
            P(None, None, "shard"),
            P(None, "shard", None),
            P(None, None, "shard"),
            P(None, "shard", None),
            P(None, None, "shard"),
            P(None, "shard", None),
            P(None, None, "shard"),
            P(None, "shard", None),
            P(None, None, "shard"),
        ),
        check_vma=False,
    )
```

profile of v0, /device:TPU:0, one launch (start us, length us, event | category | flops | bytes accessed | tf_op | source)
XLA Modules:
  0.0 1966.3 jit_solution(16018954424100614109)
XLA Ops:
  10.9 34.9 %all-gather = bf16[1,1280,16]{2,0,1:T(2,128)(2,1)S(1)} all-gather(bf16[1,160,16]{2,0,1:T(2,128)(2,1)S(1)} %copy.115), channel_id=2, replica_groups=mesh['rep'=4,'shard'=8] {'shard'}, dimensions={1}, use_global_device_ids=true | all-gather | bytes 46080 | tf_op jit(solution)/shard_map/all_gather | solution.py:193
  47.0 33.1 %all-gather.1 = bf16[1,16,1280]{1,0,2:T(2,128)(2,1)S(1)} all-gather(bf16[1,16,160]{1,0,2:T(2,128)(2,1)S(1)} %copy.116), channel_id=3, replica_groups=mesh['rep'=4,'shard'=8] {'shard'}, dimensions={2}, use_global_device_ids=true | all-gather | bytes 46080 | tf_op jit(solution)/shard_map/all_gather | solution.py:194
  92.6 33.3 %all-gather.4 = bf16[1,1280,16]{2,0,1:T(2,128)(2,1)S(1)} all-gather(bf16[1,160,16]{2,0,1:T(2,128)(2,1)S(1)} %copy.119), channel_id=6, replica_groups=mesh['rep'=4,'shard'=8] {'shard'}, dimensions={1}, use_global_device_ids=true | all-gather | bytes 46080 | tf_op jit(solution)/shard_map/all_gather | solution.py:191
  173.1 33.5 %all-gather.2 = bf16[1,1280,16]{2,0,1:T(2,128)(2,1)S(1)} all-gather(bf16[1,160,16]{2,0,1:T(2,128)(2,1)S(1)} %copy.117), channel_id=4, replica_groups=mesh['rep'=4,'shard'=8] {'shard'}, dimensions={1}, use_global_device_ids=true | all-gather | bytes 46080 | tf_op jit(solution)/shard_map/all_gather | solution.py:189
  207.7 33.4 %all-gather.3 = bf16[1,16,1280]{1,0,2:T(2,128)(2,1)S(1)} all-gather(bf16[1,16,160]{1,0,2:T(2,128)(2,1)S(1)} %copy.118), channel_id=5, replica_groups=mesh['rep'=4,'shard'=8] {'shard'}, dimensions={2}, use_global_device_ids=true | all-gather | bytes 46080 | tf_op jit(solution)/shard_map/all_gather | solution.py:190
  242.3 33.0 %all-gather.6 = bf16[1,1280,16]{2,0,1:T(2,128)(2,1)S(1)} all-gather(bf16[1,160,16]{2,0,1:T(2,128)(2,1)S(1)} %copy.121), channel_id=8, replica_groups=mesh['rep'=4,'shard'=8] {'shard'}, dimensions={1}, use_global_device_ids=true | all-gather | bytes 46080 | tf_op jit(solution)/shard_map/all_gather | solution.py:195
  276.5 33.7 %all-gather.7 = bf16[1,16,1280]{1,0,2:T(2,128)(2,1)S(1)} all-gather(bf16[1,16,160]{1,0,2:T(2,128)(2,1)S(1)} %copy.122), channel_id=9, replica_groups=mesh['rep'=4,'shard'=8] {'shard'}, dimensions={2}, use_global_device_ids=true | all-gather | bytes 46080 | tf_op jit(solution)/shard_map/all_gather | solution.py:196
  345.4 33.3 %all-gather.11 = bf16[1,16,1280]{1,0,2:T(2,128)(2,1)S(1)} all-gather(bf16[1,16,160]{1,0,2:T(2,128)(2,1)S(1)} %copy.124), channel_id=13, replica_groups=mesh['rep'=4,'shard'=8] {'shard'}, dimensions={2}, use_global_device_ids=true | all-gather | bytes 46080 | tf_op jit(solution)/shard_map/all_gather | solution.py:239
  490.6 171.9 %all-gather.33.cloned.1.call-done = bf16[1280,5120]{1,0:T(8,128)(2,1)} async-done(((bf16[160,5120]{1,0:T(8,128)(2,1)}), bf16[1280,5120]{1,0:T(8,128)(2,1)}) %all-gather.33.cloned.1.call-update) | async-done | bytes 13107216 | tf_op jit(solution)/shard_map/all_gather | solution.py:234
  679.4 166.3 %all-gather.35.cloned.1.call-done = bf16[5120,1280]{1,0:T(8,128)(2,1)} async-done(((bf16[640,1280]{1,0:T(8,128)(2,1)}), bf16[5120,1280]{1,0:T(8,128)(2,1)}) %all-gather.35.cloned.1.call-update) | async-done | bytes 13107216 | tf_op jit(solution)/shard_map/all_gather | solution.py:235
  904.7 55.5 %while.50 = (s32[]{:T(128)}, bf16[1536,16,80]{0,2,1:T(8,128)(2,1)}, bf16[1536,16,80]{0,2,1:T(8,128)(2,1)}, bf16[192,16,80]{0,2,1:T(8,128)(2,1)S(1)}, bf16[1536,1...) while((s32[]{:T(128)}, bf16[1536,16,80]{0,2,1:T(8,128)(2,1)}, ...), condition=%wide.region_14.15_spmd.clone, body=%wide.region_13.14_spmd.clone.sunk | while | flops 763725312 | bytes 20737732 | solution.py:141
  977.2 47.2 %reduce-scatter.60.cloned.1.call-done = bf16[640,16]{1,0:T(8,128)(2,1)} async-done(((bf16[5120,16]{1,0:T(8,128)(2,1)}), bf16[640,16]{1,0:T(8,128)(2,1)}) %reduce-scatter.60.cloned.1.call-update) | async-done | bytes 20496
  1025.4 65.6 %reduce-scatter.62.cloned.1.call-done = bf16[640,16]{1,0:T(8,128)(2,1)} async-done(((bf16[5120,16]{1,0:T(8,128)(2,1)}), bf16[640,16]{1,0:T(8,128)(2,1)}) %reduce-scatter.62.cloned.1.call-update) | async-done | bytes 20496
  1156.1 63.2 %reduce-scatter.54.cloned.1.call-done = bf16[160,16]{1,0:T(8,128)(2,1)} async-done(((bf16[1280,16]{1,0:T(8,128)(2,1)}), bf16[160,16]{1,0:T(8,128)(2,1)}) %reduce-scatter.54.cloned.1.call-update) | async-done | bytes 5136
  1220.1 63.4 %reduce-scatter.42.cloned.1.call-done = bf16[160,16]{1,0:T(8,128)(2,1)} async-done(((bf16[1280,16]{1,0:T(8,128)(2,1)}), bf16[160,16]{1,0:T(8,128)(2,1)}) %reduce-scatter.42.cloned.1.call-update) | async-done | bytes 5136
  1284.3 62.6 %reduce-scatter.64.cloned.1.call-done = bf16[160,16]{1,0:T(8,128)(2,1)} async-done(((bf16[1280,16]{1,0:T(8,128)(2,1)}), bf16[160,16]{1,0:T(8,128)(2,1)}) %reduce-scatter.64.cloned.1.call-update) | async-done | bytes 5136
  1347.8 62.6 %reduce-scatter.56.cloned.1.call-done = bf16[160,16]{1,0:T(8,128)(2,1)} async-done(((bf16[1280,16]{1,0:T(8,128)(2,1)}), bf16[160,16]{1,0:T(8,128)(2,1)}) %reduce-scatter.56.cloned.1.call-update) | async-done | bytes 5136
  1411.3 62.7 %reduce-scatter.44.cloned.1.call-done = bf16[160,16]{1,0:T(8,128)(2,1)} async-done(((bf16[1280,16]{1,0:T(8,128)(2,1)}), bf16[160,16]{1,0:T(8,128)(2,1)}) %reduce-scatter.44.cloned.1.call-update) | async-done | bytes 5136
  1510.9 140.2 %reduce-scatter.40.cloned.1.call-done = bf16[192,2560]{1,0:T(8,128)(2,1)} async-done(((bf16[1536,2560]{1,0:T(8,128)(2,1)}), bf16[192,2560]{1,0:T(8,128)(2,1)}) %reduce-scatter.40.cloned.1.call-update) | async-done | bytes 983056
  1669.0 46.4 %reduce-scatter.46.cloned.1.call-done = bf16[160,16]{1,0:T(8,128)(2,1)} async-done(((bf16[1280,16]{1,0:T(8,128)(2,1)}), bf16[160,16]{1,0:T(8,128)(2,1)}) %reduce-scatter.46.cloned.1.call-update) | async-done | bytes 5136
  1716.3 62.6 %reduce-scatter.50.cloned.1.call-done = bf16[160,16]{1,0:T(8,128)(2,1)} async-done(((bf16[1280,16]{1,0:T(8,128)(2,1)}), bf16[160,16]{1,0:T(8,128)(2,1)}) %reduce-scatter.50.cloned.1.call-update) | async-done | bytes 5136
  1779.7 62.8 %reduce-scatter.48.cloned.1.call-done = bf16[160,16]{1,0:T(8,128)(2,1)} async-done(((bf16[1280,16]{1,0:T(8,128)(2,1)}), bf16[160,16]{1,0:T(8,128)(2,1)}) %reduce-scatter.48.cloned.1.call-update) | async-done | bytes 5136
  1843.4 62.8 %reduce-scatter.52.cloned.1.call-done = bf16[160,16]{1,0:T(8,128)(2,1)} async-done(((bf16[1280,16]{1,0:T(8,128)(2,1)}), bf16[160,16]{1,0:T(8,128)(2,1)}) %reduce-scatter.52.cloned.1.call-update) | async-done | bytes 5136
  1910.0 34.6 %all-reduce.5.cloned.1.call-done = (bf16[8,160,16]{1,2,0:T(8,128)(2,1)}, bf16[8,16,160]{2,1,0:T(8,128)(2,1)}, bf16[8,160,16]{1,2,0:T(8,128)(2,1)}, bf16[8,16,160...) async-done(((bf16[8,160,16]{1,2,0:T(8,128)(2,1)}, ...) | async-done | bytes 409616 | tf_op jit(solution)/shard_map/psum | solution.py:356
  (416 shorter events, 558.8 us)
Async XLA Ops:
  7.2 80.6 %all-gather.21.cloned.1.call-start = ((), (), s32[]{:S(2)}) async-start(), calls=%async_computation.13 | async-start | bytes 3686400 | tf_op jit(solution)/shard_map/all_gather | solution.py:187
  7.9 158.3 %all-gather.27.cloned.1.call-start = ((), (), s32[]{:S(2)}) async-start(), calls=%async_computation.16 | async-start | bytes 3686400 | tf_op jit(solution)/shard_map/all_gather | solution.py:186
  8.7 434.8 %all-gather.25.cloned.1.call-start = ((), (), s32[]{:S(2)}) async-start(), calls=%async_computation.15 | async-start | bytes 3686400 | tf_op jit(solution)/shard_map/all_gather | solution.py:185
  9.4 437.5 %all-gather.23.cloned.1.call-start = ((), (), s32[]{:S(2)}) async-start(), calls=%async_computation.14 | async-start | bytes 4423680 | tf_op jit(solution)/shard_map/all_gather | solution.py:222
  91.7 361.5 %all-gather.29.cloned.1.call-start = ((), (), s32[]{:S(2)}) async-start(), calls=%async_computation.17 | async-start | bytes 4423680 | tf_op jit(solution)/shard_map/all_gather | solution.py:221
  170.1 316.1 %all-gather.31.cloned.1.call-start = ((), (), s32[]{:S(2)}) async-start(), calls=%async_computation.18 | async-start | bytes 3686400 | tf_op jit(solution)/shard_map/all_gather | solution.py:188
  170.7 491.8 %all-gather.33.cloned.1.call-start = ((), (), s32[]{:S(2)}) async-start(), calls=%async_computation.19 | async-start | bytes 14745600 | tf_op jit(solution)/shard_map/all_gather | solution.py:234
  171.5 674.3 %all-gather.35.cloned.1.call-start = ((), (), s32[]{:S(2)}) async-start(), calls=%async_computation.20 | async-start | bytes 14745600 | tf_op jit(solution)/shard_map/all_gather | solution.py:235
  172.2 852.2 %reduce-scatter.60.cloned.1.call-start = ((), (), s32[]{:S(2)}) async-start(), calls=%async_computation.31 | async-start | bytes 1474560
  961.7 129.3 %reduce-scatter.62.cloned.1.call-start = ((), (), s32[]{:S(2)}) async-start(), calls=%async_computation.32 | async-start | bytes 1474560
  965.5 189.7 %reduce-scatter.58.cloned.1.call-start = ((), (), s32[]{:S(2)}) async-start(), calls=%async_computation.30 | async-start | bytes 368640
  968.9 250.3 %reduce-scatter.54.cloned.1.call-start = ((), (), s32[]{:S(2)}) async-start(), calls=%async_computation.28 | async-start | bytes 368640
  971.2 312.3 %reduce-scatter.42.cloned.1.call-start = ((), (), s32[]{:S(2)}) async-start(), calls=%async_computation.22 | async-start | bytes 368640
  972.4 374.6 %reduce-scatter.64.cloned.1.call-start = ((), (), s32[]{:S(2)}) async-start(), calls=%async_computation.33 | async-start | bytes 368640
  973.6 436.9 %reduce-scatter.56.cloned.1.call-start = ((), (), s32[]{:S(2)}) async-start(), calls=%async_computation.29 | async-start | bytes 368640
  974.8 499.1 %reduce-scatter.44.cloned.1.call-start = ((), (), s32[]{:S(2)}) async-start(), calls=%async_computation.23 | async-start | bytes 368640
  977.2 530.4 %all-reduce.7.cloned.1.call-start = ((), (), s32[]{:S(2)}) async-start(), calls=%async_computation.35 | async-start | bytes 655360 | tf_op jit(solution)/shard_map/psum | solution.py:365
  1093.6 557.6 %reduce-scatter.40.cloned.1.call-start = ((), (), s32[]{:S(2)}) async-start(), calls=%async_computation.21 | async-start | bytes 8847360
  1111.3 604.1 %reduce-scatter.46.cloned.1.call-start = ((), (), s32[]{:S(2)}) async-start(), calls=%async_computation.24 | async-start | bytes 368640
  1124.5 526.6 %copy-start.27 = (bf16[1,16,1280]{2,1,0:T(8,128)(2,1)S(1)}, bf16[1,16,1280]{2,1,0:T(8,128)(2,1)}, u32[]{:S(2)}) copy-start(bf16[1,16,1280]{2,1,0:T(8,128)(2,1)} %copy-done.26) | copy-start | bytes 122884
  1653.6 125.3 %reduce-scatter.50.cloned.1.call-start = ((), (), s32[]{:S(2)}) async-start(), calls=%async_computation.26 | async-start | bytes 368640
  1662.8 179.7 %reduce-scatter.48.cloned.1.call-start = ((), (), s32[]{:S(2)}) async-start(), calls=%async_computation.25 | async-start | bytes 368640
  1665.1 241.2 %reduce-scatter.52.cloned.1.call-start = ((), (), s32[]{:S(2)}) async-start(), calls=%async_computation.27 | async-start | bytes 368640
  1668.9 275.7 %all-reduce.5.cloned.1.call-start = ((), (), s32[]{:S(2)}) async-start(), calls=%async_computation.34 | async-start | bytes 1310720 | tf_op jit(solution)/shard_map/psum | solution.py:356
  (64 other events, 3730.6 us)
Sparse Core Ops, SparseCore 0:
  10.2 77.5 all-gather.20
  90.0 76.1 all-gather.26
  168.4 79.5 all-gather.24
  250.7 87.9 all-gather.22
  341.3 73.9 all-gather.28
  417.3 61.5 all-gather.30
  481.1 181.3 all-gather.32
  664.7 180.9 all-gather.34
  961.8 62.5 reduce-scatter.59
  1027.6 63.3 reduce-scatter.61
  1094.8 60.3 reduce-scatter.57
  1158.9 60.3 reduce-scatter.53
  1223.1 60.3 reduce-scatter.41
  1286.6 60.2 reduce-scatter.63
  1350.1 60.3 reduce-scatter.55
  1413.6 60.3 reduce-scatter.43
  1476.1 31.4 all-reduce.6
  1511.1 139.9 reduce-scatter.39
  1655.0 60.3 reduce-scatter.45
  1718.5 60.3 reduce-scatter.49
  1782.2 60.3 reduce-scatter.47
  1845.8 60.3 reduce-scatter.51
  1910.4 34.1 all-reduce.4
where the time goes:
time: 1980 us; the launch traced here: 1970 us
  waiting for transfers between devices  1250 us (63%)
  blocking collectives  397 us (20%)
  matrix products  182 us (9%)
  local copies, waits for them, and re-layouts  72.1 us (4%)
  other arithmetic  45.7 us (2%)
    unnamed x36, waiting for transfers between devices  836 us
    all_gather x1, waiting for transfers between devices, body(): lax.all_gather(w_up, 'shard', axis=0, tiled=True)  172 us
    all_gather x1, waiting for transfers between devices, body(): lax.all_gather(w_down, 'shard', axis=0, tiled=True)  166 us
  transfers between devices with their start and end apart: 23, of which 19 were waited for; matrix products, arithmetic and copies ran while one was open for 8% of the time, Pallas kernels for 0%

commit v1 on v0

v1 whole, which is shorter than its diff:
```python
from functools import partial

import jax
import jax.numpy as jnp
from jax import lax
from jax.experimental import pallas as pl
from jax.experimental.pallas import tpu as pltpu
from jax.sharding import PartitionSpec as P

D = 1280
FF = 5120
HEADS = 16
HEAD = 80
LANES = 128
RANK = 16
SETS = 8
GROUP = 4

EPSILON = 1e-05
NEGATIVE = -1e30
LOG2E = 1.4426950408889634
SCALE = HEAD ** (-0.5)
ONE_LANE = HEAD
MASK_LANE = HEAD + 1

BF = jnp.bfloat16
F32 = jnp.float32


def dot(left, right):
    return jnp.dot(left, right, preferred_element_type=F32)


def dot_nt(left, right):
    return lax.dot_general(left, right, (((1,), (1,)), ((), ())), preferred_element_type=F32)


def dot_tn(left, right):
    return lax.dot_general(left, right, (((0,), (0,)), ((), ())), preferred_element_type=F32)


def norm_parts(values):
    center = values - jnp.mean(values, axis=-1, keepdims=True)
    spread = jnp.mean(center * center, axis=-1, keepdims=True)
    inverse = lax.rsqrt(spread + EPSILON)
    return center * inverse, inverse


def norm_back(grad, normal, inverse):
    average = jnp.mean(grad, axis=-1, keepdims=True)
    along = jnp.mean(grad * normal, axis=-1, keepdims=True)
    return inverse * (grad - average - normal * along)


def forward_kernel(q_ref, k_ref, v_ref, ctx_ref, lse_ref):
    scores = dot_nt(q_ref[...], k_ref[...])
    factor = SCALE * LOG2E
    highest = jnp.max(scores, axis=1, keepdims=True)
    weights = jnp.exp2((scores - highest) * factor).astype(BF)
    portion = dot(weights, v_ref[...])
    total = portion[:, ONE_LANE : ONE_LANE + 1]
    ctx_ref[...] = (portion / total).astype(BF)
    lse_ref[0] = highest * factor + jnp.log2(total)


def attend(qkv, heads_here, block):
    seq_len = qkv.shape[0]
    lanes = heads_here * LANES
    return pl.pallas_call(
        forward_kernel,
        grid=(heads_here, seq_len // block),
        in_specs=[
            pl.BlockSpec((block, LANES), lambda h, i: (i, h)),
            pl.BlockSpec((seq_len, LANES), lambda h, i: (0, heads_here + h)),
            pl.BlockSpec((seq_len, LANES), lambda h, i: (0, 2 * heads_here + h)),
        ],
        out_specs=[
            pl.BlockSpec((block, LANES), lambda h, i: (i, h)),
            pl.BlockSpec((1, block, 1), lambda h, i: (h, i, 0)),
        ],
        out_shape=[
            jax.ShapeDtypeStruct((seq_len, lanes), BF),
            jax.ShapeDtypeStruct((heads_here, seq_len, 1), F32),
        ],
        compiler_params=pltpu.CompilerParams(vmem_limit_bytes=48 << 20),
        cost_estimate=pl.CostEstimate(
            flops=4 * lanes * seq_len * seq_len,
            transcendentals=heads_here * seq_len * seq_len,
            bytes_accessed=8 * seq_len * lanes,
        ),
        name="attention_forward",
    )(qkv, qkv, qkv)


def backward_kernel(q_ref, k_ref, v_ref, do_ref, lse_ref, delta_ref, dq_ref, dk_ref, dv_ref, dq_acc):
    step = pl.program_id(1)
    queries = q_ref[...]
    keys = k_ref[...]
    douts = do_ref[...]
    scores = dot_nt(keys, queries)
    weights = jnp.exp2(scores * (SCALE * LOG2E) - lse_ref[0])
    grad_weights = dot_nt(v_ref[...], douts)
    grad_scores = (weights * (grad_weights - delta_ref[0])).astype(BF)
    dv_ref[...] = dot(weights.astype(BF), douts).astype(BF)
    dk_ref[...] = (dot(grad_scores, queries) * SCALE).astype(BF)
    part = dot_tn(grad_scores, keys)

    @pl.when(step == 0)
    def _():
        dq_acc[...] = part

    @pl.when(step > 0)
    def _():
        dq_acc[...] += part

    @pl.when(step == pl.num_programs(1) - 1)
    def _():
        dq_ref[...] = (dq_acc[...] * SCALE).astype(BF)


def attend_back(qkv, douts, lse, delta, heads_here, block):
    seq_len = qkv.shape[0]
    lanes = heads_here * LANES
    full = jax.ShapeDtypeStruct((seq_len, lanes), BF)
    return pl.pallas_call(
        backward_kernel,
        grid=(heads_here, seq_len // block),
        in_specs=[
            pl.BlockSpec((seq_len, LANES), lambda h, i: (0, h)),
            pl.BlockSpec((block, LANES), lambda h, i: (i, heads_here + h)),
            pl.BlockSpec((block, LANES), lambda h, i: (i, 2 * heads_here + h)),
            pl.BlockSpec((seq_len, LANES), lambda h, i: (0, h)),
            pl.BlockSpec((1, 1, seq_len), lambda h, i: (h, 0, 0)),
            pl.BlockSpec((1, 1, seq_len), lambda h, i: (h, 0, 0)),
        ],
        out_specs=[
            pl.BlockSpec((seq_len, LANES), lambda h, i: (0, h)),
            pl.BlockSpec((block, LANES), lambda h, i: (i, h)),
            pl.BlockSpec((block, LANES), lambda h, i: (i, h)),
        ],
        out_shape=[full, full, full],
        scratch_shapes=[pltpu.VMEM((seq_len, LANES), F32)],
        compiler_params=pltpu.CompilerParams(vmem_limit_bytes=48 << 20),
        cost_estimate=pl.CostEstimate(
            flops=10 * lanes * seq_len * seq_len,
            transcendentals=heads_here * seq_len * seq_len,
            bytes_accessed=16 * seq_len * lanes,
        ),
        name="attention_backward",
    )(qkv, qkv, qkv, douts, lse, delta)


def body(
    hidden,
    out_grad,
    clip_lengths,
    adapter_index,
    w_query,
    w_key,
    w_value,
    w_output,
    w_up,
    w_down,
    a_query,
    b_query,
    a_key,
    b_key,
    a_value,
    b_value,
    a_output,
    b_output,
    a_up,
    b_up,
    a_down,
    b_down,
):
    shards = lax.axis_size("shard")
    reps = lax.axis_size("rep")
    rows = hidden.shape[0]
    seq_len = rows * shards
    wide = D // shards
    heads_here = HEADS // shards
    lanes_here = heads_here * LANES
    ff_wide = FF // shards
    quarter = ff_wide // GROUP
    shard = lax.axis_index("shard")
    rep = lax.axis_index("rep")
    part = rep % GROUP
    length = clip_lengths[0]
    chosen = adapter_index[0]

    def mate(value, flip):
        return lax.ppermute(value, "rep", [(i, i ^ flip) for i in range(reps)])

    def pick(tables):
        return lax.dynamic_index_in_dim(tables, chosen, 0, keepdims=False)

    sets = [adapter_index] + [mate(adapter_index, flip) for flip in range(1, GROUP)]

    hidden_all = lax.all_gather(hidden, "shard", axis=0, tiled=True)
    stacked = jnp.stack((w_query, w_key, w_value), axis=1).reshape(wide, 3, shards, wide)
    qkv_cols = lax.all_to_all(
        jnp.transpose(stacked, (2, 0, 1, 3)), "shard", split_axis=0, concat_axis=0, tiled=True
    )
    qkv_cols = qkv_cols.reshape(D, 3 * heads_here, HEAD)
    qkv_cols = jnp.pad(qkv_cols, ((0, 0), (0, 0), (0, LANES - HEAD))).reshape(D, 3 * lanes_here)

    enter_pack = jnp.concatenate([pick(t) for t in (a_query, a_key, a_value, a_output, a_up)], axis=1)
    enters = lax.all_gather(enter_pack, "shard", axis=0, tiled=True)
    leave_pack = jnp.concatenate([pick(t) for t in (b_query, b_key, b_value, b_output, b_down)], axis=0)
    leaves = lax.all_gather(leave_pack, "shard", axis=1, tiled=True)
    enter_qkv = enters[:, : 3 * RANK]
    enter_o = enters[:, 3 * RANK : 4 * RANK]
    enter_u = enters[:, 4 * RANK :]
    leave_q, leave_k, leave_v, leave_o, leave_d = [leaves[i * RANK : (i + 1) * RANK] for i in range(5)]

    up_cols = lax.dynamic_index_in_dim(
        w_up.reshape(wide, shards, GROUP, quarter), part, 2, keepdims=False
    ).reshape(wide, shards * quarter)
    up_weight = lax.all_gather(up_cols, "shard", axis=0, tiled=True)
    down_rows = lax.dynamic_slice_in_dim(w_down, part * quarter, quarter, 0)
    down_weight = lax.all_gather(down_rows, "shard", axis=0, tiled=True)
    enter_d_rows = lax.dynamic_slice_in_dim(a_down, part * quarter, quarter, 1)
    leave_u_cols = lax.dynamic_slice_in_dim(b_up, part * quarter, quarter, 2)
    enter_d_pack = jnp.concatenate(
        [lax.dynamic_index_in_dim(enter_d_rows, s[0], 0, keepdims=False) for s in sets], axis=1
    )
    leave_u_pack = jnp.concatenate(
        [lax.dynamic_index_in_dim(leave_u_cols, s[0], 0, keepdims=False) for s in sets], axis=0
    )
    enter_d_all = lax.all_gather(enter_d_pack, "shard", axis=0, tiled=True)
    leave_u_all = lax.all_gather(leave_u_pack, "shard", axis=1, tiled=True)
    output_weight = lax.all_gather(w_output, "shard", axis=0, tiled=True)
    qkv_weight = lax.all_gather(
        jnp.concatenate((w_query, w_key, w_value), axis=1), "shard", axis=0, tiled=True
    )

    gi_down = dot_nt(out_grad, leave_d).astype(BF)

    def group_gather(value):
        other = mate(value, 2)
        return [value, mate(value, 1), other, mate(other, 1)]

    grads_out = group_gather(out_grad)
    gis_down = group_gather(gi_down)

    inputs_all = hidden_all.astype(F32)
    first_all = norm_parts(inputs_all)[0].astype(BF)
    inner_qkv = dot(first_all, enter_qkv).astype(BF)

    def head_lanes(matrix):
        cut = matrix.reshape(matrix.shape[0], heads_here, HEAD)
        return jnp.pad(cut, ((0, 0), (0, 0), (0, LANES - HEAD))).reshape(matrix.shape[0], lanes_here)

    zero = jnp.zeros((RANK, lanes_here), BF)
    leave_block = jnp.concatenate(
        [
            jnp.concatenate([head_lanes(pick(t)) if i == j else zero for j in range(3)], axis=1)
            for i, t in enumerate((b_query, b_key, b_value))
        ],
        axis=0,
    )
    lane = lax.broadcasted_iota(jnp.int32, (1, 3 * lanes_here), 1)
    kind = lane // lanes_here
    inside = lane % LANES
    ones = jnp.where((kind == 2) & (inside == ONE_LANE) | (kind == 0) & (inside == MASK_LANE), 1.0, 0.0)
    bias = jnp.where(jnp.arange(seq_len)[:, None] < length, 0.0, NEGATIVE)
    extra = ones + jnp.where((kind == 1) & (inside == MASK_LANE), bias, 0.0)
    qkv = (dot(first_all, qkv_cols) + dot(inner_qkv, leave_block) + extra).astype(BF)
    ctx_heads, lse = attend(qkv, heads_here, 256)

    def drop_lanes(matrix):
        return matrix.reshape(seq_len, heads_here, LANES)[:, :, :HEAD].reshape(shards, rows, wide)

    def to_tokens(matrix):
        moved = lax.all_to_all(drop_lanes(matrix), "shard", split_axis=0, concat_axis=0, tiled=True)
        return jnp.transpose(moved, (1, 0, 2)).reshape(rows, D)

    context = to_tokens(ctx_heads)

    inputs = hidden.astype(F32)
    first, first_inverse = norm_parts(inputs)
    inner_o = dot(context, enter_o).astype(BF)
    middle = inputs + dot(context, output_weight) + dot(inner_o, leave_o)
    second, second_inverse = norm_parts(middle)
    second_b = second.astype(BF)
    inner_u = dot(second_b, enter_u).astype(BF)

    seconds = group_gather(second_b)
    inners_u = group_gather(inner_u)
    leave_us = [leave_u_all[i * RANK : (i + 1) * RANK] for i in range(GROUP)]
    enter_ds = [enter_d_all[:, i * RANK : (i + 1) * RANK] for i in range(GROUP)]

    def join(pieces):
        return jnp.concatenate(pieces, axis=0)

    def cut(matrix):
        return [matrix[i * rows : (i + 1) * rows] for i in range(GROUP)]

    pre_act = dot(join(seconds), up_weight) + join([dot(i, l) for i, l in zip(inners_u, leave_us)])
    cumulative = 0.5 * (1.0 + lax.erf(pre_act * (0.5**0.5)))
    density = jnp.exp(-0.5 * pre_act * pre_act) * (0.5 / jnp.pi) ** 0.5
    activated = (pre_act * cumulative).astype(BF)
    acts = cut(activated)
    mlp_parts = cut(dot(activated, down_weight).astype(BF))
    down_parts = [dot(a, e).astype(BF) for a, e in zip(acts, enter_ds)]
    grad_act = dot_nt(join(grads_out), down_weight) + join(
        [dot_nt(g, e) for g, e in zip(gis_down, enter_ds)]
    )
    grad_pre = (grad_act * (cumulative + pre_act * density)).astype(BF)
    grad_pres = cut(grad_pre)
    h2_parts = cut(dot_nt(grad_pre, up_weight).astype(BF))
    gi_up_parts = [dot_nt(g, l).astype(BF) for g, l in zip(grad_pres, leave_us)]
    ga_down = [dot_tn(a, g) for a, g in zip(acts, gis_down)]
    gb_up = [dot_tn(g, i) for g, i in zip(grad_pres, inners_u)]

    def group_reduce(pieces):
        near = pieces[0].astype(F32) + mate(pieces[1], 1).astype(F32)
        far = (pieces[2].astype(F32) + mate(pieces[3], 1).astype(F32)).astype(BF)
        return near + mate(far, 2).astype(F32)

    inner_d = group_reduce(down_parts).astype(BF)
    mlp = group_reduce(mlp_parts) + dot(inner_d, leave_d)
    layer_out = (middle + mlp).astype(BF)
    gb_down = dot_tn(out_grad, inner_d)
    gi_up = group_reduce(gi_up_parts).astype(BF)
    grad_second = group_reduce(h2_parts) + dot_nt(gi_up, enter_u)
    ga_up = dot_tn(second_b, gi_up)
    grad_middle = out_grad.astype(F32) + norm_back(grad_second, second, second_inverse)
    grad_attn = grad_middle.astype(BF)
    gb_output = dot_tn(grad_attn, inner_o)
    gi_output = dot_nt(grad_attn, leave_o).astype(BF)
    ga_output = dot_tn(context, gi_output)
    grad_context = (dot_nt(grad_attn, output_weight) + dot_nt(gi_output, enter_o)).astype(BF)

    moved = jnp.transpose(grad_context.reshape(rows, shards, wide), (1, 0, 2))
    moved = lax.all_to_all(moved, "shard", split_axis=0, concat_axis=0, tiled=True)
    douts = head_lanes(moved.reshape(seq_len, wide))
    delta = jnp.sum(
        (douts.astype(F32) * ctx_heads.astype(F32)).reshape(seq_len, heads_here, LANES), axis=2
    )
    delta = jnp.transpose(delta)[:, None, :]
    grads = attend_back(qkv, douts, lse.reshape(heads_here, 1, seq_len), delta, heads_here, 256)
    gb_heads = [
        jnp.transpose(
            dot_tn(g, inner_qkv[:, i * RANK : (i + 1) * RANK]).reshape(heads_here, LANES, RANK)[:, :HEAD], (2, 0, 1)
        ).reshape(RANK, wide)
        for i, g in enumerate(grads)
    ]
    joined = jnp.concatenate([drop_lanes(g) for g in grads], axis=2)
    joined = lax.all_to_all(joined, "shard", split_axis=0, concat_axis=0, tiled=True)
    grad_qkv = jnp.transpose(joined.reshape(shards, rows, 3, wide), (1, 2, 0, 3)).reshape(rows, 3 * D)
    first_b = first.astype(BF)
    gis = [
        dot_nt(grad_qkv[:, i * D : (i + 1) * D], l).astype(BF)
        for i, l in enumerate((leave_q, leave_k, leave_v))
    ]
    gi_qkv = jnp.concatenate(gis, axis=1)
    ga_qkv = dot_tn(first_b, gi_qkv)
    grad_first = dot_nt(grad_qkv, qkv_weight) + dot_nt(gi_qkv, enter_qkv)
    input_grad = (grad_middle + norm_back(grad_first, first, first_inverse)).astype(BF)

    pieces = jnp.concatenate([ga_qkv, ga_output, ga_up, gb_output, gb_down] + ga_down + gb_up, axis=1)
    pieces = pieces.astype(BF).reshape(shards, wide, -1)
    pieces = lax.all_to_all(pieces, "shard", split_axis=0, concat_axis=0, tiled=True)
    pieces = jnp.sum(pieces.astype(F32), axis=0)
    heads_t = jnp.transpose(jnp.concatenate(gb_heads, axis=0))
    pieces = jnp.concatenate([pieces, heads_t], axis=1).astype(BF)
    gathered = lax.all_gather(pieces, "rep", axis=0, tiled=False).astype(F32)
    indices = lax.all_gather(adapter_index, "rep", axis=0, tiled=True)
    hot = (indices[:, None] == jnp.arange(SETS)[None, :]).astype(F32)

    def own(slot):
        return jnp.einsum(
            "cs,cir->sir", hot, gathered[:, :, slot * RANK : (slot + 1) * RANK], precision=lax.Precision.HIGHEST
        )

    def turned(matrix):
        return jnp.transpose(matrix, (0, 2, 1))

    def split(first_slot):
        outs = []
        for q in range(GROUP):
            total = 0.0
            for base in range(0, reps, GROUP):
                device = base + q
                for k in range(GROUP):
                    slot = first_slot + k
                    piece = gathered[device, :, slot * RANK : (slot + 1) * RANK]
                    total = total + hot[device ^ k][:, None, None] * piece[None]
            outs.append(total)
        return jnp.concatenate(outs, axis=1)

    return (
        layer_out,
        input_grad,
        own(0),
        turned(own(15)),
        own(1),
        turned(own(16)),
        own(2),
        turned(own(17)),
        own(3),
        turned(own(5)),
        own(4),
        turned(split(11)),
        split(7),
        turned(own(6)),
    )


def solution(mesh):
    rows = P("shard", None)
    enter = P(None, "shard", None)
    leave = P(None, None, "shard")
    tokens = P(("rep", "shard"), None)
    return jax.shard_map(
        body,
        mesh=mesh,
        in_specs=(tokens, tokens, P("rep"), P("rep")) + (rows,) * 6 + (enter, leave) * 6,
        out_specs=(tokens, tokens) + (enter, leave) * 6,
        check_vma=False,
    )
```

time: 1980 us -> 604 us (0.31)
  waiting for transfers between devices: 1250 us -> 76.9 us
  blocking collectives: 397 us -> 198 us
  matrix products: 182 us -> 81.4 us
  local copies, waits for them, and re-layouts: 72.1 us -> 122 us
  starting transfers between devices: 0.93 us -> 39.3 us
  Pallas kernels: 0 us -> 27.9 us
    unnamed x36 -> x5, waiting for transfers between devices: 836 us -> 1.43 us
    all_gather x8 -> x5, waiting for transfers between devices: 349 us -> 0.05 us  [the longest x1 0.02 us: body(): lax.all_gather(jnp.concatenate((w_query, w_key, w_value), axis=1), 'shard...]
    all_gather x12 -> x5, blocking collectives: 397 us -> 194 us  [the longest x1 76.2 us: body(): enters = lax.all_gather(enter_pack, 'shard', axis=0, tiled=True)]
    dot_general x80 -> x64, matrix products: 182 us -> 81.4 us  [the longest x18 35.9 us: dot(): return jnp.dot(left, right, preferred_element_type=F32)]
    psum x2 -> x0, waiting for transfers between devices: 67.5 us -> none  [the longest x1 34.6 us: body(): lax.psum(placed[0].astype(jnp.bfloat16), 'rep').astype(jnp.float32)]
    all_to_all x0 -> x5, waiting for transfers between devices: none -> 49.5 us  [the longest x1 27 us: body(): lax.all_to_all(moved, 'shard', split_axis=0, concat_axis=0, tiled=True)]
    pallas_call x0 -> x2, Pallas kernels: none -> 27.9 us  [the longest x1 17.1 us: attend_back(): pl.pallas_call(backward_kernel, grid=(heads_here, seq_len // block), in_s...]
    reshape x0 -> x24, local copies, waits for them, and re-layouts: none -> 27.8 us  [the longest x9 14.6 us: drop_lanes(): matrix.reshape(seq_len, heads_here, LANES)[:, :, :HEAD]]
  transfers between devices with their start and end apart: 23 -> 37, of which waited for: 19 -> 8; matrix products, arithmetic and copies ran while one was open for 8% -> 36% of each run, Pallas kernels for 0% -> 5%
where the time goes in v1:
time: 604 us; the launch traced here: 594 us
  blocking collectives  198 us (33%)
  local copies, waits for them, and re-layouts  122 us (20%)
  matrix products  81.4 us (13%)
  waiting for transfers between devices  76.9 us (13%)
  starting transfers between devices  39.3 us (7%)
  Pallas kernels  27.9 us (5%)
  other arithmetic  26.1 us (4%)
  between operations  22.4 us (4%)
    all_gather x1, blocking collectives, body(): enters = lax.all_gather(enter_pack, 'shard', axis=0, tiled=True)  76.2 us
    all_gather x1, blocking collectives, body(): leave_u_all = lax.all_gather(leave_u_pack, 'shard', axis=1, tiled=True)  46.7 us
    dot_general x18, matrix products, dot(): return jnp.dot(left, right, preferred_element_type=F32)  35.9 us
    all_gather x1, blocking collectives, body(): leaves = lax.all_gather(leave_pack, 'shard', axis=1, tiled=True)  32.6 us
    dot_general x20, matrix products, dot_nt(): lax.dot_general(left, right, (((1,), (1,)), ((), ())), preferred_element_...  32.1 us
    all_gather x1, blocking collectives, body(): enter_d_all = lax.all_gather(enter_d_pack, 'shard', axis=0, tiled=True)  31.8 us
    all_to_all x1, waiting for transfers between devices, body(): lax.all_to_all(moved, 'shard', split_axis=0, concat_axis=0, tiled=True)  27 us
    ppermute x27, waiting for transfers between devices, mate(): return lax.ppermute(value, 'rep', [(i, i ^ flip) for i in range(reps)])  25.9 us
  transfers between devices with their start and end apart: 37, of which 8 were waited for; matrix products, arithmetic and copies ran while one was open for 36% of the time, Pallas kernels for 5%

profile of v1, /device:TPU:0, one launch (start us, length us, event | category | flops | bytes accessed | tf_op | source)
XLA Modules:
  0.0 593.9 jit_solution(13392343024341315223)
XLA Ops:
  8.7 5.2 reshape.343
  14.0 5.9 dynamic-slice_reduce_fusion
  29.0 32.6 %all_gather.37 = bf16[80,1280]{0,1:T(8,128)(2,1)S(1)} all-gather(bf16[80,160]{0,1:T(8,128)(2,1)S(1)} %concatenate.105), channel_id=1, replica_groups=mesh['rep'=4,'shard'=8] {'shard'}, dimensions={1}, use_global_device_ids=true | all-gather | bytes 230400 | tf_op jit(solution)/shard_map/all_gather | solution.py:211
  68.9 5.7 all-to-all-start
  81.0 4.3 all-reduce.7
  85.4 76.2 %all_gather.35 = bf16[1280,80]{1,0:T(8,128)(2,1)S(1)} all-gather(bf16[160,80]{1,0:T(8,128)(2,1)S(1)} %concatenate.100), channel_id=1, replica_groups=mesh['rep'=4,'shard'=8] {'shard'}, dimensions={0}, use_global_device_ids=true | all-gather | bytes 230400 | tf_op jit(solution)/shard_map/all_gather | solution.py:209
  171.8 31.8 %all-gather.1 = bf16[8,160,64]{1,2,0:T(8,128)(2,1)S(1)} all-gather(bf16[1,160,64]{1,2,0:T(8,128)(2,1)S(1)} %maximum_bitcast_fusion.3), channel_id=1, replica_groups=mesh['rep'=4,'shard'=8] {'shard'}, dimensions={0}, use_global_device_ids=true | all-gather | bytes 184320 | tf_op jit(solution)/shard_map/all_gather | solution.py:231
  227.6 10.8 %attention_forward.1 = (bf16[1536,256]{1,0:T(8,128)(2,1)S(1)}, f32[2,1536,1]{2,1,0:T(8,128)S(1)}) custom-call(bf16[1536,768]{1,0:T(8,128)(2,1)S(1)} %add_convert_fusion.q_ref.k_ref.v_ref, bf16[1536,768]{1,0:T(8,128)(2,1)S(1)} %add_convert_fusion.q_ref.k_ref.v_ref, bf16[1536,768]{1,0:T(8,128)(2,1)S(1)} %add_convert_fusion.q_ref.k_ref.v_ref), custom_call_target="tpu_custom_call" | custom-call | flops 2415919104 | bytes 3145728 | tf_op jit(solution)/shard_map/attention_forward/pallas_call | solution.py:69
  245.8 4.2 all-to-all-start.1
  250.8 46.7 %all-gather = bf16[8,160,64]{1,2,0:T(8,128)(2,1)S(1)} all-gather(bf16[1,160,64]{1,2,0:T(8,128)(2,1)S(1)} %maximum_bitcast_fusion.2), channel_id=1, replica_groups=mesh['rep'=4,'shard'=8] {'shard'}, dimensions={0}, use_global_device_ids=true | all-gather | bytes 184320 | tf_op jit(solution)/shard_map/all_gather | solution.py:232
  319.1 8.4 %collective-permute-done.1 = bf16[192,1280]{1,0:T(8,128)(2,1)} collective-permute-done((bf16[192,1280]{1,0:T(8,128)(2,1)S(1)}, bf16[192,1280]{1,0:T(8,128)(2,1)}, u32[]{:S(2)}, u32[]{:S(2)}) %collective-permute-start.1) | collective-permute-done | bytes 491552 | tf_op jit(solution)/shard_map/ppermute | solution.py:193
  330.0 8.8 %multiply_convert_fusion = (bf16[768,1280]{1,0:T(8,128)(2,1)}, f32[768,1280]{1,0:T(8,128)}) fusion(f32[192,1280]{1,0:T(8,128)} %fusion.116, f32[192,1280]{1,0:T(8,128)} %fusion.119, f32[192,1280]{1,0:T(8,128)} %fusion.122, f32[192,1280]{1,0:T(8,128)} %fusion.125, bf16[1280,1280]{1,0:T(8,128)(2,1)} %all-gather.12.cloned.1.call-done, ...), kind=kOutput, calls=%fused_computation.16 | convolution fusion | flops 2533294080 | bytes 15073280 | tf_op jit(solution)/shard_map/dot_general | solution.py:31
  338.9 7.2 %fusion.9 = bf16[768,1280]{1,0:T(8,128)(2,1)S(1)} fusion(f32[768,1280]{1,0:T(8,128)} %get-tuple-element.153, f32[192,1280]{1,0:T(8,128)} %fusion.103, f32[192,1280]{1,0:T(8,128)} %fusion.106, f32[192,1280]{1,0:T(8,128)} %fusion.109, f32[192,1280]{1,0:T(8,128)} %fusion.112, bf16[1280,1280]{1,0:T(8,128)(2,1)} %all-gather.14.cloned.1.call-done, ...), kind=kOutput, calls=%fused_computation.13 | convolution fusion | flops 2538209280 | bytes 15073280 | tf_op jit(solution)/shard_map/dot_general | solution.py:35
  362.5 9.6 %collective-permute-done.26 = bf16[192,16]{0,1:T(8,128)(2,1)S(1)} collective-permute-done((bf16[192,16]{0,1:T(8,128)(2,1)S(1)}, bf16[192,16]{0,1:T(8,128)(2,1)S(1)}, u32[]{:S(2)}, u32[]{:S(2)}) %collective-permute-start.26) | collective-permute-done | bytes 6176 | tf_op jit(solution)/shard_map/ppermute | solution.py:193
  390.3 27.0 %all-to-all-done.2 = bf16[8,192,160]{1,2,0:T(8,128)(2,1)S(1)} async-done(((bf16[8,192,160]{1,2,0:T(8,128)(2,1)}), bf16[8,192,160]{1,2,0:T(8,128)(2,1)S(1)}, u32[]{:S(2)}, u32[]{:S(2)}) %all-to-all-start.2) | async-done | bytes 491552 | tf_op jit(solution)/shard_map/all_to_all | solution.py:337
  426.6 17.1 %attention_backward.1 = (bf16[1536,256]{1,0:T(8,128)(2,1)S(1)}, bf16[1536,256]{1,0:T(8,128)(2,1)S(1)}, bf16[1536,256]{1,0:T(8,128)(2,1)S(1)}) custom-call(bf16[1536,768]{1,0:T(8,128)(2,1)S(1)} %copy-done.3, bf16[1536,768]{1,0:T(8,128)(2,1)S(1)} %copy-done.3, bf16[1536,768]{1,0:T(8,128)(2,1)S(1)} %copy-done.3, bf16[1536,256]{1,0:T(8,128)(2,1)S(1)} %copy.205.do_ref, ...), custom_call_target="tpu_custom_call" | custom-call | flops 6039797760 | bytes 6291456 | tf_op jit(solution)/shard_map/attention_backward/pallas_call | solution.py:125
  460.1 4.5 copy.133
  464.6 4.6 all-to-all-start.3
  490.7 6.5 %collective-permute-done.11 = bf16[192,1280]{1,0:T(8,128)(2,1)} collective-permute-done((bf16[192,1280]{1,0:T(8,128)(2,1)}, bf16[192,1280]{1,0:T(8,128)(2,1)}, u32[]{:S(2)}, u32[]{:S(2)}) %collective-permute-start.11) | collective-permute-done | bytes 491552 | tf_op jit(solution)/shard_map/ppermute | solution.py:193
  500.1 5.9 all-to-all-done.3
  513.4 4.9 concatenate.127
  522.9 16.6 %all-to-all-done.4 = bf16[8,160,240]{2,1,0:T(8,128)(2,1)S(1)} async-done(((bf16[8,160,240]{2,1,0:T(8,128)(2,1)}), bf16[8,160,240]{2,1,0:T(8,128)(2,1)S(1)}, u32[]{:S(2)}, u32[]{:S(2)}) %all-to-all-start.4) | async-done | bytes 614432 | tf_op jit(solution)/shard_map/all_to_all | solution.py:365
  539.7 6.8 %all_gather.44 = bf16[4,160,288]{2,1,0:T(8,128)(2,1)S(1)} all-gather(bf16[1,160,288]{2,1,0:T(8,128)(2,1)S(1)} %pad_maximum_fusion.3), channel_id=1, replica_groups=mesh['rep'=4,'shard'=8] {'rep'}, dimensions={0}, use_global_device_ids=true | all-gather | bytes 460800 | tf_op jit(solution)/shard_map/all_gather | solution.py:369
  576.9 7.8 %fusion.183 = f32[192,1280]{1,0:T(8,128)S(1)} fusion(bf16[192,3840]{0,1:T(8,128)(2,1)} %bitcast.300, bf16[1280,3840]{1,0:T(8,128)(2,1)} %all-gather.16.cloned.1.call-done), kind=kOutput, calls=%fused_computation.331 | convolution fusion | flops 1887436800 | bytes 12288000 | tf_op jit(solution)/shard_map/dot_general | solution.py:35
  (455 shorter events, 212.4 us)
Async XLA Ops:
  7.2 208.6 %all-gather.8.cloned.1.call-start = ((), (), s32[]{:S(2)}) async-start(), calls=%async_computation.5 | async-start | bytes 4423680 | tf_op jit(solution)/shard_map/all_gather | solution.py:200
  7.9 301.2 %all-gather.10.cloned.1.call-start = ((), (), s32[]{:S(2)}) async-start(), calls=%async_computation.6 | async-start | bytes 3686400 | tf_op jit(solution)/shard_map/all_gather | solution.py:233
  8.7 321.4 %all-gather.12.cloned.1.call-start = ((), (), s32[]{:S(2)}) async-start(), calls=%async_computation.7 | async-start | bytes 3686400 | tf_op jit(solution)/shard_map/all_gather | solution.py:220
  21.3 317.5 %all-gather.14.cloned.1.call-start = ((), (), s32[]{:S(2)}) async-start(), calls=%async_computation.8 | async-start | bytes 3686400 | tf_op jit(solution)/shard_map/all_gather | solution.py:222
  22.2 141.1 %collective-permute-start.3 = (s32[1]{0:T(128)}, s32[1]{0:T(128)}, u32[]{:S(2)}, u32[]{:S(2)}) collective-permute-start(s32[1]{0:T(128)} %param.25), channel_id=1, source_target_pairs={{0,8},{8,0},{16,24},{24,16},{1,9},{9,1},{17,25},{25,17},{2,10},{10... | collective-permute-start | bytes 20 | tf_op jit(solution)/shard_map/ppermute | solution.py:193
  22.8 143.5 %collective-permute-start.4 = (s32[1]{0:T(128)}, s32[1]{0:T(128)}, u32[]{:S(2)}, u32[]{:S(2)}) collective-permute-start(s32[1]{0:T(128)} %param.25), channel_id=1, source_target_pairs={{0,16},{8,24},{16,0},{24,8},{1,17},{9,25},{17,1},{25,9},{2,18},{10... | collective-permute-start | bytes 20 | tf_op jit(solution)/shard_map/ppermute | solution.py:193
  25.4 142.3 %collective-permute-start.5 = (s32[1]{0:T(128)}, s32[1]{0:T(128)}, u32[]{:S(2)}, u32[]{:S(2)}) collective-permute-start(s32[1]{0:T(128)} %param.25), channel_id=1, source_target_pairs={{0,24},{8,16},{16,8},{24,0},{1,25},{9,17},{17,9},{25,1},{2,26},{10... | collective-permute-start | bytes 20 | tf_op jit(solution)/shard_map/ppermute | solution.py:193
  63.1 237.2 %collective-permute-start.19 = (bf16[192,16]{0,1:T(8,128)(2,1)S(1)}, bf16[192,16]{0,1:T(8,128)(2,1)S(1)}, u32[]{:S(2)}, u32[]{:S(2)}) collective-permute-start(bf16[192,16]{0,1:T(8,128)(2,1)S(1)} %bitcast.333), channel_id=1, source_target_pairs={{0,16},{8,24},{16,0},{24,8},{1,17},{9,25},{17,1},{25,9},{2,18},{10... | collective-permute-start | bytes 18440 | tf_op jit(solution)/shard_map/ppermute | solution.py:193
  64.5 237.8 %collective-permute-start.18 = (bf16[192,16]{0,1:T(8,128)(2,1)S(1)}, bf16[192,16]{0,1:T(8,128)(2,1)}, u32[]{:S(2)}, u32[]{:S(2)}) collective-permute-start(bf16[192,16]{0,1:T(8,128)(2,1)S(1)} %bitcast.334), channel_id=1, source_target_pairs={{0,8},{8,0},{16,24},{24,16},{1,9},{9,1},{17,25},{25,17},{2,10},{10... | collective-permute-start | bytes 18440 | tf_op jit(solution)/shard_map/ppermute | solution.py:193
  68.9 137.9 %all-to-all-start = ((bf16[8,160,3,160]{1,3,2,0:T(8,128)(2,1)}), bf16[8,160,3,160]{1,3,2,0:T(8,128)(2,1)}, u32[]{:S(2)}, u32[]{:S(2)}) async-start(bf16[8,160,3,160]{1,3,2,0:T(8,128)(2,1)} %maximum_bitcast_fusion), calls=%async_computation | async-start | bytes 3932160 | tf_op jit(solution)/shard_map/all_to_all | solution.py:202
  74.6 502.2 %all-gather.16.cloned.1.call-start = ((), (), s32[]{:S(2)}) async-start(), calls=%async_computation.9 | async-start | bytes 11059200 | tf_op jit(solution)/shard_map/all_gather | solution.py:234
  163.3 143.2 %collective-permute-start.16 = (bf16[192,1280]{1,0:T(8,128)(2,1)}, bf16[192,1280]{1,0:T(8,128)(2,1)}, u32[]{:S(2)}, u32[]{:S(2)}) collective-permute-start(bf16[192,1280]{1,0:T(8,128)(2,1)} %param.23), channel_id=1, source_target_pairs={{0,16},{8,24},{16,0},{24,8},{1,17},{9,25},{17,1},{25,9},{2,18},{10... | collective-permute-start | bytes 1474568 | tf_op jit(solution)/shard_map/ppermute | solution.py:193
  166.3 172.5 %collective-permute-start.15 = (bf16[192,1280]{1,0:T(8,128)(2,1)}, bf16[192,1280]{1,0:T(8,128)(2,1)}, u32[]{:S(2)}, u32[]{:S(2)}) collective-permute-start(bf16[192,1280]{1,0:T(8,128)(2,1)} %param.23), channel_id=1, source_target_pairs={{0,8},{8,0},{16,24},{24,16},{1,9},{9,1},{17,25},{25,17},{2,10},{10... | collective-permute-start | bytes 1474568 | tf_op jit(solution)/shard_map/ppermute | solution.py:193
  245.8 61.7 %all-to-all-start.1 = ((bf16[8,192,160]{1,2,0:T(8,128)(2,1)}), bf16[8,192,160]{1,2,0:T(8,128)(2,1)}, u32[]{:S(2)}, u32[]{:S(2)}) async-start(bf16[8,192,160]{1,2,0:T(8,128)(2,1)} %copy.116), calls=%async_computation.1 | async-start | bytes 1310720 | tf_op jit(solution)/shard_map/all_to_all | solution.py:276
  306.5 32.3 %collective-permute-start.17 = (bf16[192,1280]{1,0:T(8,128)(2,1)}, bf16[192,1280]{1,0:T(8,128)(2,1)}, u32[]{:S(2)}, u32[]{:S(2)}) collective-permute-start(bf16[192,1280]{1,0:T(8,128)(2,1)} %collective-permute-done.16), channel_id=1, source_target_pairs={{0,8},{8,0},{16,24},{24,16},{1,9},{9,1},{17,25},{25,17},{2,10},{10... | collective-permute-start | bytes 1474568 | tf_op jit(solution)/shard_map/ppermute | solution.py:193
  313.6 13.8 %collective-permute-start.1 = (bf16[192,1280]{1,0:T(8,128)(2,1)S(1)}, bf16[192,1280]{1,0:T(8,128)(2,1)}, u32[]{:S(2)}, u32[]{:S(2)}) collective-permute-start(bf16[192,1280]{1,0:T(8,128)(2,1)S(1)} %fusion.41), channel_id=1, source_target_pairs={{0,16},{8,24},{16,0},{24,8},{1,17},{9,25},{17,1},{25,9},{2,18},{10... | collective-permute-start | bytes 1474568 | tf_op jit(solution)/shard_map/ppermute | solution.py:193
  350.2 21.9 %collective-permute-start.21 = (bf16[192,1280]{1,0:T(8,128)(2,1)S(1)}, bf16[192,1280]{1,0:T(8,128)(2,1)S(1)}, u32[]{:S(2)}, u32[]{:S(2)}) collective-permute-start(bf16[192,1280]{1,0:T(8,128)(2,1)S(1)} %get-tuple-element.84), channel_id=1, source_target_pairs={{0,8},{8,0},{16,24},{24,16},{1,9},{9,1},{17,25},{25,17},{2,10},{10... | collective-permute-start | bytes 1474568 | tf_op jit(solution)/shard_map/ppermute | solution.py:193
  351.7 122.9 %collective-permute-start.13 = (bf16[192,16]{0,1:T(8,128)(2,1)}, bf16[192,16]{0,1:T(8,128)(2,1)}, u32[]{:S(2)}, u32[]{:S(2)}) collective-permute-start(bf16[192,16]{0,1:T(8,128)(2,1)} %convolution_convert_fusion.30), channel_id=1, source_target_pairs={{0,8},{8,0},{16,24},{24,16},{1,9},{9,1},{17,25},{25,17},{2,10},{10... | collective-permute-start | bytes 18440 | tf_op jit(solution)/shard_map/ppermute | solution.py:193
  358.7 13.5 %collective-permute-start.23 = (bf16[192,1280]{1,0:T(8,128)(2,1)S(1)}, bf16[192,1280]{1,0:T(8,128)(2,1)S(1)}, u32[]{:S(2)}, u32[]{:S(2)}) collective-permute-start(bf16[192,1280]{1,0:T(8,128)(2,1)S(1)} %add_convert_fusion.1), channel_id=1, source_target_pairs={{0,16},{8,24},{16,0},{24,8},{1,17},{9,25},{17,1},{25,9},{2,18},{10... | collective-permute-start | bytes 1474568 | tf_op jit(solution)/shard_map/ppermute | solution.py:193
  362.5 116.1 %collective-permute-start.12 = (bf16[192,16]{0,1:T(8,128)(2,1)}, bf16[192,16]{0,1:T(8,128)(2,1)}, u32[]{:S(2)}, u32[]{:S(2)}) collective-permute-start(bf16[192,16]{0,1:T(8,128)(2,1)} %convolution_convert_fusion.32), channel_id=1, source_target_pairs={{0,8},{8,0},{16,24},{24,16},{1,9},{9,1},{17,25},{25,17},{2,10},{10... | collective-permute-start | bytes 18440 | tf_op jit(solution)/shard_map/ppermute | solution.py:193
  378.1 39.3 %all-to-all-start.2 = ((bf16[8,192,160]{1,2,0:T(8,128)(2,1)}), bf16[8,192,160]{1,2,0:T(8,128)(2,1)S(1)}, u32[]{:S(2)}, u32[]{:S(2)}) async-start(bf16[8,192,160]{1,2,0:T(8,128)(2,1)} %bitcast.38), calls=%async_computation.2 | async-start | bytes 1310720 | tf_op jit(solution)/shard_map/all_to_all | solution.py:337
  464.6 41.4 %all-to-all-start.3 = ((bf16[8,192,480]{2,1,0:T(8,128)(2,1)}), bf16[8,192,480]{2,1,0:T(8,128)(2,1)}, u32[]{:S(2)}, u32[]{:S(2)}) async-start(bf16[8,192,480]{2,1,0:T(8,128)(2,1)} %copy.133), calls=%async_computation.3 | async-start | bytes 3145728 | tf_op jit(solution)/shard_map/all_to_all | solution.py:351
  474.1 16.6 %collective-permute-start.9 = (bf16[192,1280]{1,0:T(8,128)(2,1)}, bf16[192,1280]{1,0:T(8,128)(2,1)}, u32[]{:S(2)}, u32[]{:S(2)}) collective-permute-start(bf16[192,1280]{1,0:T(8,128)(2,1)} %get-tuple-element.86), channel_id=1, source_target_pairs={{0,8},{8,0},{16,24},{24,16},{1,9},{9,1},{17,25},{25,17},{2,10},{10... | collective-permute-start | bytes 1474568 | tf_op jit(solution)/shard_map/ppermute | solution.py:193
  518.4 21.1 %all-to-all-start.4 = ((bf16[8,160,240]{2,1,0:T(8,128)(2,1)}), bf16[8,160,240]{2,1,0:T(8,128)(2,1)S(1)}, u32[]{:S(2)}, u32[]{:S(2)}) async-start(bf16[8,160,240]{2,1,0:T(8,128)(2,1)} %concatenate.127), calls=%async_computation.4 | async-start | bytes 1310720 | tf_op jit(solution)/shard_map/all_to_all | solution.py:365
  (78 other events, 1321.2 us)
Sparse Core Ops, SparseCore 0:
  10.2 82.2 all-gather.7
  94.7 85.4 all-gather.9
  182.9 61.0 all-gather.11
  246.0 67.6 all-gather.13
  315.7 152.9 all-gather.15

commit v2 on v1

v2 whole, which is shorter than its diff:
```python
import jax
import jax.numpy as jnp
from jax import lax
from jax.experimental import pallas as pl
from jax.experimental.pallas import tpu as pltpu
from jax.sharding import PartitionSpec as P

D = 1280
FF = 5120
HEADS = 16
HEAD = 80
LANES = 128
RANK = 16
SETS = 8
GROUP = 4
FOLD = 4
CHUNK = 256
TAIL = D + LANES
RATE = 1.15e9

EPSILON = 1e-05
NEGATIVE = -1e30
LOG2E = 1.4426950408889634
SCALE = HEAD ** (-0.5)
ONE_LANE = HEAD
MASK_LANE = HEAD + 1

BF = jnp.bfloat16
F32 = jnp.float32

QUARTER = D // GROUP
ENTER_QKV = 0
ENTER_O = 48
ENTER_U = 64
LEAVE_O = 80
LEAVE_D = 96
FIRST = 128
BESIDE = 512
BUNDLE = D + BESIDE

ENTER_D = 0
LEAVE_U = 64
LEAVE_QKV = 128
LATE = 256

SHARD, PART, LENGTH, CORE, RING = range(5)

VMEM = pl.BlockSpec(memory_space=pltpu.VMEM)
SMEM = pl.BlockSpec(memory_space=pltpu.SMEM)
ANY = pl.BlockSpec(memory_space=pl.ANY)


def dot(left, right):
    return jnp.dot(left, right, preferred_element_type=F32)


def dot_nt(left, right):
    return lax.dot_general(left, right, (((1,), (1,)), ((), ())), preferred_element_type=F32)


def dot_tn(left, right):
    return lax.dot_general(left, right, (((0,), (0,)), ((), ())), preferred_element_type=F32)


def norm_parts(values):
    center = values - jnp.mean(values, axis=-1, keepdims=True)
    spread = jnp.mean(center * center, axis=-1, keepdims=True)
    inverse = lax.rsqrt(spread + EPSILON)
    return center * inverse, inverse


def norm_back(grad, normal, inverse):
    average = jnp.mean(grad, axis=-1, keepdims=True)
    along = jnp.mean(grad * normal, axis=-1, keepdims=True)
    return inverse * (grad - average - normal * along)


def cost(micros):
    return pl.CostEstimate(flops=int(micros * RATE), transcendentals=0, bytes_accessed=0)


def call(kernel, name, outs, ins, specs, out_specs=None, scratch=(), micros=1.0, **rest):
    return pl.pallas_call(
        kernel,
        out_shape=outs,
        in_specs=specs,
        out_specs=[VMEM] * len(outs) if out_specs is None else out_specs,
        scratch_shapes=list(scratch),
        compiler_params=pltpu.CompilerParams(vmem_limit_bytes=56 << 20),
        cost_estimate=cost(micros),
        name=name,
        **rest,
    )(*ins)


def shape(*dims, dtype=BF):
    return jax.ShapeDtypeStruct(dims, dtype)


def padded(size):
    return -(-size // LANES) * LANES


def column_blocks(wq, wk, wv, shards):
    wide = D // shards
    pad = jnp.zeros((wide, padded(3 * wide) - 3 * wide), BF)
    for s in range(shards):
        at = slice(s * wide, (s + 1) * wide)
        yield s, jnp.concatenate([wq[:, at], wk[:, at], wv[:, at], pad], axis=1)


def pack_columns(meta, weights, after, shards):
    wide = D // shards
    slot = padded(3 * wide)
    count = shards // GROUP

    def kernel(meta, wq, wk, wv, after, cols, quarter):
        for s, block in column_blocks(wq, wk, wv, shards):
            cols[s] = jnp.where(meta[CORE] == 0, block[:, : slot // 2], block[:, slot // 2 :])

            @pl.when(meta[PART] == s // count)
            def _():
                quarter[:, s % count * slot : (s % count + 1) * slot] = block

    outs = [shape(shards, wide, slot // 2), shape(wide, count * slot)]
    return call(kernel, "pack_columns", outs, (meta, *weights, after), [SMEM] + [VMEM] * 3 + [ANY], micros=3)


def unit(size):
    row = lax.broadcasted_iota(jnp.int32, (size, size), 0)
    col = lax.broadcasted_iota(jnp.int32, (size, size), 1)
    return (row == col).astype(BF)


def pack_first(chosen, meta, hidden, w_output, narrow):
    rows = hidden.shape[0]
    wide = narrow[0].shape[2]

    def kernel(chosen, meta, hidden, w_output, *refs):
        out = refs[-1]
        eye = unit(wide)
        out[:, :D] = hidden[...]
        out[:, D:] = jnp.zeros((rows, BESIDE), BF)
        for i, ref in enumerate(refs[:-1]):
            out[:wide, D + i * RANK : D + (i + 1) * RANK] = dot_nt(eye, ref[...]).astype(BF)
        for p in range(GROUP):

            @pl.when(meta[PART] == p)
            def _():
                out[:wide, D + FIRST : D + FIRST + QUARTER] = w_output[:, p * QUARTER : (p + 1) * QUARTER]

    return pl.pallas_call(
        kernel,
        out_shape=shape(rows, BUNDLE),
        grid_spec=pltpu.PrefetchScalarGridSpec(
            num_scalar_prefetch=1,
            grid=(1,),
            in_specs=[SMEM, pl.BlockSpec((rows, D), lambda i, m: (0, 0)), pl.BlockSpec((wide, D), lambda i, m: (0, 0))]
            + [pl.BlockSpec((None, RANK, wide), lambda i, m: (m[0], 0, 0))] * len(narrow),
            out_specs=pl.BlockSpec((rows, BUNDLE), lambda i, m: (0, 0)),
        ),
        cost_estimate=cost(3),
        name="pack_first",
    )(chosen, meta, hidden, w_output, *narrow)


def feed_kernel(*refs, wide, shards):
    part = refs[GROUP][0]
    (w_up, w_down), maps, (out, rows_down, sem) = refs[GROUP + 1 : GROUP + 3], refs[GROUP + 3 : -4], refs[-3:]
    narrow, downs, ups = maps[:3], maps[3:7], maps[7:11]
    copy = pltpu.make_async_copy(w_down.at[part], rows_down, sem)
    copy.start()
    eye = unit(wide)
    beside = D
    for i, ref in enumerate(narrow):
        start = beside + LEAVE_QKV + i * RANK
        out[:, start : start + RANK] = dot_nt(eye, ref[...]).astype(BF)
    end = beside + LEAVE_QKV + 3 * RANK
    out[:, end:] = jnp.zeros((wide, D + LATE - end), BF)
    for p in range(GROUP):

        @pl.when(part == p)
        def _():
            at = slice(p * wide, (p + 1) * wide)
            for i, ref in enumerate(downs):
                start = beside + ENTER_D + i * RANK
                out[:, start : start + RANK] = dot_nt(eye, ref[:, at]).astype(BF)
            for i, ref in enumerate(ups):
                start = beside + LEAVE_U + i * RANK
                out[:, start : start + RANK] = dot_nt(eye, ref[:, at]).astype(BF)
            for s in range(shards):
                start = (s * GROUP + p) * wide
                out[:, s * wide : (s + 1) * wide] = w_up[:, start : start + wide]

    copy.wait()


def pack_feed(sets, part, w_up, w_down, narrow, a_down, b_up, after, shards):
    wide = D // shards
    ff_wide = GROUP * wide
    width = D + LATE

    def at(k):
        return lambda i, *m: (m[k][0], 0, 0)

    specs = (
        [pl.BlockSpec((wide, FF), lambda i, *m: (0, 0)), ANY]
        + [pl.BlockSpec((None, RANK, wide), at(0))] * 3
        + [pl.BlockSpec((None, RANK, ff_wide), at(k)) for k in range(GROUP)] * 2
        + [ANY]
    )

    def kernel(*refs):
        feed_kernel(*refs, wide=wide, shards=shards)

    return pl.pallas_call(
        kernel,
        out_shape=[shape(wide, width), shape(wide, D)],
        grid_spec=pltpu.PrefetchScalarGridSpec(
            num_scalar_prefetch=GROUP + 1,
            grid=(1,),
            in_specs=specs,
            out_specs=[pl.BlockSpec((wide, n), lambda i, *m: (0, 0)) for n in (width, D)],
            scratch_shapes=[pltpu.SemaphoreType.DMA],
        ),
        cost_estimate=cost(5),
        name="pack_feed",
    )(*sets, part, w_up, w_down.reshape(GROUP, wide, D), *narrow, *[a_down] * GROUP, *[b_up] * GROUP, after)


def ring_shard(place, shards):
    return jnp.where(place < shards // 2, 2 * place, 2 * (shards - 1 - place) + 1)


def ring_pieces(value, shards, between):
    places = [2 * i if i < shards // 2 else 2 * (shards - 1 - i) + 1 for i in range(shards)]
    onward = [(places[i], places[(i + 1) % shards]) for i in range(shards)]
    back = [(b, a) for a, b in onward]
    half = value.shape[0] // 2
    pieces = [(value, 0, 0)]
    below, above = value, value
    for k in range(1, shards // 2):
        below = lax.ppermute(below, "shard", onward)
        above = lax.ppermute(above, "shard", back)
        below, above = between(k, (below, above))
        pieces += [(below, -k, 0), (above, k, 0)]
    far = shards // 2
    pieces.append((lax.ppermute(below[:half], "shard", onward), far, 0))
    pieces.append((lax.ppermute(above[half:], "shard", back), far, half))
    return pieces


def piece_shard(meta, step, shards):
    return ring_shard((meta[RING] + step + shards) % shards, shards)


def place_pieces(meta, pieces, steps, target, sems):
    shards = target.shape[0]
    copies = []
    for i, (ref, (step, start)) in enumerate(zip(pieces, steps)):
        block = target.at[piece_shard(meta, step, shards), pl.ds(start, ref.shape[0])]
        copies.append(pltpu.make_async_copy(ref, block, sems.at[i]))
    for copy in copies:
        copy.start()
    for copy in copies:
        copy.wait()


def qkv_kernel(meta, w_mine, w_mate, *refs, shards, steps):
    count = len(steps)
    pieces, leaves = refs[:count], refs[count : count + 3]
    first_ref, qkv_ref, inner_ref, enter, quarter, hid, sems = refs[-7:]
    wide = D // shards
    heads_here = HEADS // shards
    slot = padded(3 * wide)
    side = meta[CORE]
    rows = hid.shape[1]
    place_pieces(meta, pieces, steps, hid, sems)
    for s in range(shards):
        enter[s * wide : (s + 1) * wide, :] = hid[s, :wide, D : D + FIRST]
        quarter[s * wide : (s + 1) * wide, :] = hid[s, :wide, D + FIRST : D + FIRST + QUARTER]
    lane = lax.broadcasted_iota(jnp.int32, (rows, LANES - HEAD), 1)
    spot = lax.broadcasted_iota(jnp.int32, (rows, LANES - HEAD), 0)

    def step(s, carry):
        at = pl.ds(pl.multiple_of(s * rows, 64), rows)
        first = norm_parts(hid[s, :, :D].astype(F32))[0].astype(BF)
        first_ref[at, :] = first
        inner = dot(first, enter[:, : 3 * RANK]).astype(BF)
        inner_ref[at, :] = inner
        y_mine = dot(first, w_mine[...].reshape(D, slot // 2))
        y_mate = dot(first, w_mate[...].reshape(D, slot // 2))
        lo = jnp.where(side == 0, y_mine, y_mate)
        hi = jnp.where(side == 0, y_mate, y_mine)
        y = jnp.concatenate([lo, hi], axis=1)
        hidden_key = jnp.where((spot + s * rows < meta[LENGTH]) | (lane != MASK_LANE - HEAD), 0.0, NEGATIVE)
        for kind in range(3):
            lanes = slice(kind * RANK, (kind + 1) * RANK)
            out = y[:, kind * wide : (kind + 1) * wide] + dot(inner[:, lanes], leaves[kind][...])
            if kind == 0:
                tail = jnp.where(lane == MASK_LANE - HEAD, 1.0, 0.0)
            elif kind == 1:
                tail = hidden_key
            else:
                tail = jnp.where(lane == ONE_LANE - HEAD, 1.0, 0.0)
            for h in range(heads_here):
                base = (kind * heads_here + h) * LANES
                head = jnp.concatenate([out[:, h * HEAD : (h + 1) * HEAD], tail], axis=1)
                qkv_ref[at, base : base + LANES] = head.astype(BF)
        return carry

    lax.fori_loop(0, shards, step, 0)


def project_qkv(meta, chosen, w_mine, w_mate, pieces, leaves):
    shards = len(pieces) - 1
    steps = [p[1:] for p in pieces]
    rows = pieces[0][0].shape[0]
    seq_len = rows * shards
    lanes = HEADS // shards * LANES
    wide = D // shards
    weight = pl.BlockSpec(w_mine.shape, lambda i, c: (0, 0, 0))
    outs = [
        shape(seq_len, D),
        shape(seq_len, 3 * lanes),
        shape(seq_len, 3 * RANK),
        shape(D, FIRST),
        shape(D, QUARTER),
    ]

    def kernel(chosen, *refs):
        qkv_kernel(*refs, shards=shards, steps=steps)

    return pl.pallas_call(
        kernel,
        out_shape=outs,
        grid_spec=pltpu.PrefetchScalarGridSpec(
            num_scalar_prefetch=1,
            grid=(1,),
            in_specs=[SMEM, weight, weight]
            + [ANY] * len(pieces)
            + [pl.BlockSpec((None, RANK, wide), lambda i, c: (c[0], 0, 0))] * 3,
            out_specs=[pl.BlockSpec(o.shape, lambda i, c: (0, 0)) for o in outs],
            scratch_shapes=[
                pltpu.VMEM((shards, rows, BUNDLE), BF),
                pltpu.SemaphoreType.DMA((len(pieces),)),
            ],
        ),
        compiler_params=pltpu.CompilerParams(vmem_limit_bytes=56 << 20),
        cost_estimate=cost(14),
        name="project_qkv",
    )(chosen, meta, w_mine, w_mate, *[p[0] for p in pieces], *leaves)


def forward_kernel(qkv_ref, *refs, heads_here, wide):
    packed_ref, ctx_ref, lse_ref = refs[-3:]
    rows = ctx_ref.shape[0]
    part = rows // FOLD
    at = pl.ds(pl.multiple_of(pl.program_id(0) * rows, 64), rows)
    factor = SCALE * LOG2E
    for h in range(heads_here):
        queries = qkv_ref[at, h * LANES : (h + 1) * LANES]
        keys = qkv_ref[:, (heads_here + h) * LANES : (heads_here + h + 1) * LANES]
        values = qkv_ref[:, (2 * heads_here + h) * LANES : (2 * heads_here + h + 1) * LANES]
        scores = dot_nt(queries, keys)
        highest = jnp.max(scores, axis=1, keepdims=True)
        weights = jnp.exp2((scores - highest) * factor).astype(BF)
        portion = dot(weights, values)
        total = portion[:, ONE_LANE : ONE_LANE + 1]
        context = (portion / total).astype(BF)
        ctx_ref[:, h * LANES : (h + 1) * LANES] = context
        lse_ref[h] = highest * factor + jnp.log2(total)
        for g in range(FOLD):
            start = g * wide + h * HEAD
            packed_ref[0, :, start : start + HEAD] = context[g * part : (g + 1) * part, :HEAD]


def attend(qkv, shards):
    seq_len = qkv.shape[0]
    rows = seq_len // shards
    heads_here = HEADS // shards
    lanes = heads_here * LANES
    wide = D // shards

    def kernel(*refs):
        forward_kernel(*refs, heads_here=heads_here, wide=wide)

    return call(
        kernel,
        "attention_forward",
        [
            shape(shards, rows // FOLD, FOLD * wide),
            shape(seq_len, lanes),
            shape(heads_here, seq_len, 1, dtype=F32),
        ],
        (qkv,),
        [pl.BlockSpec((seq_len, 3 * lanes), lambda d: (0, 0))],
        out_specs=[
            pl.BlockSpec((1, rows // FOLD, FOLD * wide), lambda d: (d, 0, 0)),
            pl.BlockSpec((rows, lanes), lambda d: (d, 0)),
            pl.BlockSpec((heads_here, rows, 1), lambda d: (0, d, 0)),
        ],
        micros=12,
        grid=(shards,),
    )


def backward_kernel(
    qkv_ref, moved_ref, ctx_ref, lse_ref, first, inner, leave_q, leave_k, leave_v, out_ref, heads_ref, douts, delta, acc,
    *, heads_here, wide, block
):
    shards = moved_ref.shape[0]
    seq_len = qkv_ref.shape[0]
    rows = seq_len // shards
    part = rows // FOLD
    slot = out_ref.shape[2]
    for d in range(shards):
        for g in range(FOLD):
            base = d * rows + g * part
            for h in range(heads_here):
                start = g * wide + h * HEAD
                piece = moved_ref[d, :, start : start + HEAD]
                douts[base : base + part, h * LANES : h * LANES + HEAD] = piece
    for h in range(heads_here):
        douts[:, h * LANES + HEAD : (h + 1) * LANES] = jnp.zeros((seq_len, LANES - HEAD), BF)
    ones = jnp.ones((8, LANES), F32)
    if slot > 3 * wide:
        out_ref[:, :, 3 * wide :] = jnp.zeros((shards, rows + RANK, slot - 3 * wide), BF)
    for h in range(heads_here):
        lanes = slice(h * LANES, (h + 1) * LANES)
        product = douts[:, lanes].astype(F32) * ctx_ref[:, lanes].astype(F32)
        delta[...] = lax.dot_general(
            ones, product, (((1,), (1,)), ((), ())), precision=lax.Precision.HIGHEST, preferred_element_type=F32
        )
        queries = qkv_ref[:, lanes]
        grads = douts[:, lanes]

        def step(i, carry):
            at = pl.ds(pl.multiple_of(i * block, block), block)
            keys = qkv_ref[at, (heads_here + h) * LANES : (heads_here + h + 1) * LANES]
            values = qkv_ref[at, (2 * heads_here + h) * LANES : (2 * heads_here + h + 1) * LANES]
            scores = dot_nt(keys, queries)
            weights = jnp.exp2(scores * (SCALE * LOG2E) - lse_ref[h])
            grad_weights = dot_nt(values, grads)
            grad_scores = (weights * (grad_weights - delta[0:1, :])).astype(BF)
            acc[2, at, :] = dot(weights.astype(BF), grads)
            acc[1, at, :] = dot(grad_scores, queries) * SCALE
            moved = dot_tn(grad_scores, keys)

            @pl.when(i == 0)
            def _():
                acc[0] = moved

            @pl.when(i > 0)
            def _():
                acc[0] += moved

            return carry

        lax.fori_loop(0, seq_len // block, step, 0)
        for kind in range(3):
            start = kind * wide + h * HEAD
            for d in range(shards):
                piece = acc[kind, d * rows : (d + 1) * rows, :HEAD]
                if kind == 0:
                    piece = piece * SCALE
                out_ref[d, :rows, start : start + HEAD] = piece.astype(BF)
    heads_ref[...] = jnp.zeros_like(heads_ref)
    parts = []
    for kind, leave in enumerate((leave_q, leave_k, leave_v)):
        grad = out_ref[:, :rows, kind * wide : (kind + 1) * wide].reshape(seq_len, wide)
        lanes = slice(kind * RANK, (kind + 1) * RANK)
        parts.append(dot_nt(grad, leave[...]))
        heads_ref[:, kind * wide : (kind + 1) * wide] = dot_tn(inner[:, lanes], grad).astype(BF)
    entered = dot_tn(jnp.concatenate(parts, axis=1).astype(BF), first[...]).astype(BF)
    for kind in range(3):
        for d in range(shards):
            piece = entered[kind * RANK : (kind + 1) * RANK, d * wide : (d + 1) * wide]
            out_ref[d, rows:, kind * wide : (kind + 1) * wide] = piece


def attend_back(chosen, qkv, moved, ctx, lse, first, inner, leaves, after, shards):
    seq_len = qkv.shape[0]
    rows = seq_len // shards
    heads_here = HEADS // shards
    lanes = heads_here * LANES
    wide = D // shards
    outs = [shape(shards, rows + RANK, padded(3 * wide)), shape(RANK, padded(3 * wide))]

    def kernel(chosen, *refs):
        backward_kernel(*refs[:9], *refs[10:], heads_here=heads_here, wide=wide, block=256)

    def whole(array):
        return pl.BlockSpec(array.shape, lambda i, c: (0,) * len(array.shape))

    return pl.pallas_call(
        kernel,
        out_shape=outs,
        grid_spec=pltpu.PrefetchScalarGridSpec(
            num_scalar_prefetch=1,
            grid=(1,),
            in_specs=[whole(x) for x in (qkv, moved, ctx, lse, first, inner)]
            + [pl.BlockSpec((None, RANK, wide), lambda i, c: (c[0], 0, 0))] * 3
            + [ANY],
            out_specs=[whole(o) for o in outs],
            scratch_shapes=[
                pltpu.VMEM((seq_len, lanes), BF),
                pltpu.VMEM((8, seq_len), F32),
                pltpu.VMEM((3, seq_len, LANES), F32),
            ],
        ),
        compiler_params=pltpu.CompilerParams(vmem_limit_bytes=56 << 20),
        cost_estimate=cost(24),
        name="attention_backward",
    )(chosen, qkv, moved, ctx, lse, first, inner, *leaves, after)


def by_part(part, values):
    ordered = []
    for b in range(GROUP):
        total = values[0]
        for k in range(1, GROUP):
            total = jnp.where((part ^ k) == b, values[k], total)
        ordered.append(total)
    return ordered


def output_kernel(meta, moved, w0, w1, w2, w3, adapters, hidden, out_grad, *refs):
    ctx_ref, middle_ref, cat_ref, inner_ref = refs[-4:]
    shards, part, lanes = moved.shape
    wide = lanes // FOLD
    for s in range(shards):
        for g in range(FOLD):
            ctx_ref[g * part : (g + 1) * part, s * wide : (s + 1) * wide] = moved[s, :, g * wide : (g + 1) * wide]
    context = ctx_ref[...]
    inner = dot(context, adapters[:, ENTER_O : ENTER_O + RANK]).astype(BF)
    inner_ref[...] = inner
    branch = jnp.concatenate(by_part(meta[PART], [dot(context, w[...]) for w in (w0, w1, w2, w3)]), axis=1)
    branch = branch + dot_nt(inner, adapters[:, LEAVE_O : LEAVE_O + RANK])
    middle = hidden[...].astype(F32) + branch
    middle_ref[...] = middle
    second = norm_parts(middle)[0].astype(BF)
    cat_ref[:, :D] = second
    inner_u = dot(second, adapters[:, ENTER_U : ENTER_U + RANK])
    gi_down = dot(out_grad[...], adapters[:, LEAVE_D : LEAVE_D + RANK])
    empty = jnp.zeros((second.shape[0], LANES - 2 * RANK), F32)
    cat_ref[:, D:] = jnp.concatenate([inner_u, gi_down, empty], axis=1).astype(BF)


def project_output(meta, moved, weights, adapters, hidden, out_grad):
    rows = hidden.shape[0]
    return call(
        output_kernel,
        "project_output",
        [shape(rows, D), shape(rows, D, dtype=F32), shape(rows, TAIL), shape(rows, RANK)],
        (meta, moved, *weights, adapters, hidden, out_grad),
        [SMEM] + [VMEM] * 8,
        micros=6,
    )


def feed_spec(index, width=D):
    return pl.BlockSpec((D, width), lambda i: (0, index))


def down_back(meta, pieces, grads):
    arrays = [p[0] for p in pieces]
    steps = [p[1:] for p in pieces]
    count = len(arrays)
    shards, wide = count - 1, arrays[0].shape[0]
    rows = grads[0].shape[0]

    def kernel(meta, *refs):
        given, (out, weight, joined, sems) = refs[count : count + GROUP], refs[count + GROUP :]
        for k in range(GROUP):
            joined[k * rows : (k + 1) * rows] = given[k][...]
        place_pieces(meta, refs[:count], steps, weight, sems)
        for n in range(D // CHUNK):
            at = slice(n * CHUNK, (n + 1) * CHUNK)
            out[:, at] = dot_nt(joined[...], weight[...].reshape(D, D)[at, :])

    return call(
        kernel,
        "down_backward",
        [shape(GROUP * rows, D, dtype=F32), shape(shards, wide, D)],
        (meta, *arrays, *grads),
        [SMEM] + [ANY] * count + [VMEM] * GROUP,
        scratch=[pltpu.VMEM((GROUP * rows, D), BF), pltpu.SemaphoreType.DMA((count,))],
        micros=7,
    )


def up_kernel(w_ref, grad_ref, adapters, *refs):
    cats, (act_ref, pre_ref, keep, send, joined) = refs[:GROUP], refs[GROUP:]
    rows = cats[0].shape[0]
    for k in range(GROUP):
        joined[k * rows : (k + 1) * rows] = cats[k][:, :D]

    def step(n, carry):
        lanes = pl.ds(pl.multiple_of(n * CHUNK, CHUNK), CHUNK)
        weight = w_ref[:, lanes]
        pre = dot(joined[...], weight)
        extra, extra_grad = [], []
        for k in range(GROUP):
            leave = adapters[lanes, LEAVE_U + k * RANK : LEAVE_U + (k + 1) * RANK]
            enter = adapters[lanes, ENTER_D + k * RANK : ENTER_D + (k + 1) * RANK]
            extra.append(dot_nt(cats[k][:, D : D + RANK], leave))
            extra_grad.append(dot_nt(cats[k][:, D + RANK : D + 2 * RANK], enter))
        pre = pre + jnp.concatenate(extra, axis=0)
        grad = grad_ref[:, lanes] + jnp.concatenate(extra_grad, axis=0)
        cumulative = 0.5 * (1.0 + lax.erf(pre * (0.5**0.5)))
        density = jnp.exp2(pre * pre * (-0.5 * LOG2E)) * 0.3989422804014327
        act_ref[:, lanes] = (pre * cumulative).astype(BF)
        pre_ref[:, lanes] = (grad * (cumulative + pre * density)).astype(BF)
        return carry

    lax.fori_loop(0, D // CHUNK, step, 0)
    weight = w_ref[...]
    for k in range(GROUP):
        target = send if k % 2 else keep
        at = slice(k * rows, (k + 1) * rows)
        target[k // 2, :, :D] = dot_nt(pre_ref[at], weight).astype(BF)
        gi = dot(pre_ref[at], adapters[:, LEAVE_U + k * RANK : LEAVE_U + (k + 1) * RANK])
        empty = jnp.zeros((rows, LANES - RANK), F32)
        target[k // 2, :, D:] = jnp.concatenate([gi, empty], axis=1).astype(BF)


def up_both(ff, grad, cats):
    rows = cats[0].shape[0]
    total = GROUP * rows
    bundle = shape(2, rows, TAIL)
    return call(
        up_kernel,
        "up_forward_backward",
        [shape(total, D), shape(total, D), bundle, bundle],
        (ff, grad, ff, *cats),
        [feed_spec(0), pl.BlockSpec((total, D), lambda i: (0, 0)), feed_spec(D // LATE, LATE)]
        + [pl.BlockSpec((rows, TAIL), lambda i: (0, 0))] * GROUP,
        out_specs=[pl.BlockSpec((total, D), lambda i: (0, 0))] * 2
        + [pl.BlockSpec((2, rows, TAIL), lambda i: (0, 0, 0))] * 2,
        scratch=[pltpu.VMEM((total, D), BF)],
        micros=15,
        grid=(1,),
    )


def down_kernel(w_ref, act_ref, pre_ref, adapters, *refs):
    tails, (keep, send, pieces) = refs[:GROUP], refs[GROUP:]
    rows = tails[0].shape[0]
    weight = w_ref[...].reshape(D, D)
    for k in range(GROUP):
        target = send if k % 2 else keep
        at = slice(k * rows, (k + 1) * rows)
        act = act_ref[at]
        target[k // 2, :, :D] = dot(act, weight).astype(BF)
        inner = dot(act, adapters[:, ENTER_D + k * RANK : ENTER_D + (k + 1) * RANK])
        empty = jnp.zeros((rows, LANES - RANK), F32)
        target[k // 2, :, D:] = jnp.concatenate([inner, empty], axis=1).astype(BF)
        pieces[k * RANK : (k + 1) * RANK] = dot_tn(tails[k][:, RANK : 2 * RANK], act).astype(BF)
        start = (GROUP + k) * RANK
        pieces[start : start + RANK] = dot_tn(tails[k][:, :RANK], pre_ref[at]).astype(BF)


def down_forward(weight, ff, act, pre, cats):
    rows = cats[0].shape[0]
    total = GROUP * rows
    bundle = shape(2, rows, TAIL)
    return call(
        down_kernel,
        "down_forward",
        [bundle, bundle, shape(2 * GROUP * RANK, D)],
        (weight, act, pre, ff, *cats),
        [
            pl.BlockSpec(weight.shape, lambda i: (0, 0, 0)),
            pl.BlockSpec((total, D), lambda i: (0, 0)),
            pl.BlockSpec((total, D), lambda i: (0, 0)),
            feed_spec(D // LATE, LATE),
        ]
        + [pl.BlockSpec((rows, LANES), lambda i: (0, D // LANES))] * GROUP,
        out_specs=[pl.BlockSpec((2, rows, TAIL), lambda i: (0, 0, 0))] * 2
        + [pl.BlockSpec((2 * GROUP * RANK, D), lambda i: (0, 0))],
        micros=9,
        grid=(1,),
    )


def middle_kernel(
    meta, keep, near, far, middle, out_grad, w0, w1, w2, w3, adapters, grad_ref, packed, attn_ref, gi_up_ref, gi_o_ref
):
    shards, part, lanes = packed.shape
    wide = lanes // FOLD
    total = keep[0].astype(F32) + near[0].astype(F32) + far[...].astype(F32)
    gi_up = total[:, D : D + RANK].astype(BF)
    gi_up_ref[...] = gi_up
    grad = total[:, :D] + dot_nt(gi_up, adapters[:, ENTER_U : ENTER_U + RANK])
    second, inverse = norm_parts(middle[...])
    grad_middle = out_grad[...].astype(F32) + norm_back(grad, second, inverse)
    grad_ref[...] = grad_middle
    attn = grad_middle.astype(BF)
    attn_ref[...] = attn
    gi_o = dot(attn, adapters[:, LEAVE_O : LEAVE_O + RANK]).astype(BF)
    gi_o_ref[...] = gi_o
    parts = [attn[:, b * QUARTER : (b + 1) * QUARTER] for b in range(GROUP)]
    context = 0.0
    for k, w in enumerate((w0, w1, w2, w3)):
        chosen = parts[0]
        for b in range(1, GROUP):
            chosen = jnp.where((meta[PART] ^ k) == b, parts[b], chosen)
        context = context + dot_nt(chosen, w[...])
    context = (context + dot_nt(gi_o, adapters[:, ENTER_O : ENTER_O + RANK])).astype(BF)
    for s in range(shards):
        for g in range(FOLD):
            packed[s, :, g * wide : (g + 1) * wide] = context[g * part : (g + 1) * part, s * wide : (s + 1) * wide]


def middle_back(meta, keep, near, far, middle, out_grad, weights, adapters, shards):
    rows = middle.shape[0]
    wide = D // shards
    return call(
        middle_kernel,
        "middle_backward",
        [
            shape(rows, D, dtype=F32),
            shape(shards, rows // FOLD, FOLD * wide),
            shape(rows, D),
            shape(rows, RANK),
            shape(rows, RANK),
        ],
        (meta, keep, near, far, middle, out_grad, *weights, adapters),
        [SMEM] + [VMEM] * 10,
        micros=7,
    )


def scatter_stack(stack, natural):
    shards, height, _ = natural.shape
    wide = D // shards
    if natural.shape[2] > 3 * wide:
        natural[:, :, 3 * wide :] = jnp.zeros((shards, height, natural.shape[2] - 3 * wide), BF)
    for d in range(shards):
        for m in range(3 * height // RANK):
            piece = stack[m * RANK : (m + 1) * RANK, d * wide : (d + 1) * wide]
            natural[d, m // 3 * RANK : (m // 3 + 1) * RANK, m % 3 * wide : (m % 3 + 1) * wide] = piece


def token_kernel(meta, keep, near, far, middle, out_grad, adapters, cat, gi_up, context, gi_o, attn, inner_o, *refs):
    pieces, layer_ref, natural, stack = refs
    total = keep[0].astype(F32) + near[0].astype(F32) + far[...].astype(F32)
    inner_d = total[:, D : D + RANK].astype(BF)
    mlp = total[:, :D] + dot_nt(inner_d, adapters[:, LEAVE_D : LEAVE_D + RANK])
    layer_ref[...] = (middle[...] + mlp).astype(BF)
    width = pieces.shape[0]
    stack[:width] = pieces[...]
    pairs = ((gi_o[...], context[...]), (gi_up[...], cat[:, :D]), (inner_o[...], attn[...]), (inner_d, out_grad[...]))
    for i, (left, right) in enumerate(pairs):
        stack[width + i * RANK : width + (i + 1) * RANK] = dot_tn(left, right).astype(BF)
    scatter_stack(stack, natural)


def token_grads(meta, *args, shards):
    block = (4 * RANK, padded(3 * D // shards))
    rows = args[3].shape[0]
    return call(
        token_kernel,
        "token_adapter_grads",
        [shape(rows, D), shape(shards, *block)],
        (meta, *args),
        [SMEM] + [VMEM] * len(args),
        scratch=[pltpu.VMEM((12 * RANK, D), BF)],
        micros=4,
    )


def sum_pieces(moved, heads):
    rows = moved.shape[1] - RANK

    def kernel(moved, heads, out):
        out[:RANK] = jnp.sum(moved[:, rows:, :].astype(F32), axis=0).astype(BF)
        out[RANK:] = heads[...]

    return call(kernel, "sum_adapter_grads", [shape(2 * RANK, heads.shape[1])], (moved, heads), [VMEM] * 2)[0]


def input_kernel(meta, moved, w0, w1, w2, w3, adapters, late, hidden, grad_ref, after, out_ref, *, wide):
    shards, slot = moved.shape[0], moved.shape[2]
    rows = hidden.shape[0]
    count = shards // GROUP
    gis = [0.0, 0.0, 0.0]
    for s in range(shards):
        block = moved[s, :rows]
        for kind in range(3):
            bt = late[s * wide : (s + 1) * wide, LEAVE_QKV + kind * RANK : LEAVE_QKV + (kind + 1) * RANK]
            gis[kind] = gis[kind] + dot(block[:, kind * wide : (kind + 1) * wide], bt)
    gi = jnp.concatenate(gis, axis=1).astype(BF)
    grad = dot_nt(gi, adapters[:, ENTER_QKV : ENTER_QKV + 3 * RANK])
    for k, w in enumerate((w0, w1, w2, w3)):
        for j in range(count):
            place = (meta[PART] ^ k) * count + j
            grad = grad + dot_nt(moved[place, :rows], w[:, j * slot : (j + 1) * slot])
    first, inverse = norm_parts(hidden[...].astype(F32))
    out_ref[...] = (grad_ref[...] + norm_back(grad, first, inverse)).astype(BF)


def input_back(meta, moved, weights, adapters, ff, hidden, grad_middle, after, shards):
    rows = hidden.shape[0]
    wide = D // shards

    def kernel(*refs):
        input_kernel(*refs, wide=wide)

    return call(
        kernel,
        "input_backward",
        [shape(rows, D)],
        (meta, moved, *weights, adapters, ff, hidden, grad_middle, after),
        [SMEM]
        + [pl.BlockSpec(x.shape, lambda i, n=x.ndim: (0,) * n) for x in (moved, *weights, adapters)]
        + [feed_spec(D // LATE, LATE)]
        + [pl.BlockSpec(x.shape, lambda i: (0, 0)) for x in (hidden, grad_middle)]
        + [ANY],
        out_specs=[pl.BlockSpec((rows, D), lambda i: (0, 0))],
        grid=(1,),
        micros=10,
    )[0]


def spread_tokens_kernel(part, *refs, reps, wide):
    sets, blocks, (ao, bo, au, bu, ad, bd) = refs[:reps], refs[reps : 2 * reps], refs[2 * reps :]
    this = pl.program_id(0)
    flags = [jnp.where(sets[k][0] == this, 1.0, 0.0) for k in range(reps)]

    def one(value, m):
        row, lane = m // 3 * RANK, m % 3 * wide
        return value[row : row + RANK, lane : lane + wide]

    own = 0.0
    quarters = [0.0] * GROUP
    for k in range(reps):
        block = blocks[k][...].astype(F32)
        own = own + flags[k] * block[2 * RANK :]
        for j in range(GROUP):
            pair = jnp.concatenate([one(block, j), one(block, GROUP + j)], axis=0)
            quarters[k % GROUP] = quarters[k % GROUP] + flags[k ^ j] * pair
    ordered = by_part(part[0], quarters)
    ad[0] = jnp.concatenate([q[:RANK] for q in ordered], axis=1)
    bu[0] = jnp.concatenate([q[RANK:] for q in ordered], axis=1)
    for i, ref in enumerate((ao, au, bo, bd)):
        ref[0] = one(own, 2 + i)


def spread_heads_kernel(*refs, reps, wide):
    sets, blocks, outs = refs[:reps], refs[reps : 2 * reps], refs[2 * reps + 1 :]
    this = pl.program_id(0)
    own = 0.0
    for k in range(reps):
        own = own + jnp.where(sets[k][0] == this, 1.0, 0.0) * blocks[k][...].astype(F32)
    for kind in range(3):
        lanes = slice(kind * wide, (kind + 1) * wide)
        outs[2 * kind][0] = own[:RANK, lanes]
        outs[2 * kind + 1][0] = own[RANK:, lanes]


def spread(kernel, name, ins, scalars, blocks, kinds, micros, rest=0):
    outs = call(
        kernel,
        name,
        [shape(SETS, *k, dtype=F32) for k in kinds],
        ins,
        [SMEM] * scalars + [pl.BlockSpec(b.shape, lambda e: (0, 0)) for b in blocks] + [ANY] * rest,
        out_specs=[pl.BlockSpec((1, *k), lambda e: (e, 0, 0)) for k in kinds],
        micros=micros,
        grid=(SETS,),
    )
    return [jnp.transpose(o, (0, 2, 1)) if i % 2 == 0 else o for i, o in enumerate(outs)]


def spread_tokens(part, sets, blocks, wide):
    reps = len(blocks)
    narrow, broad = (RANK, wide), (RANK, GROUP * wide)

    def kernel(*refs):
        spread_tokens_kernel(*refs, reps=reps, wide=wide)

    kinds = [narrow] * 3 + [broad, broad, narrow]
    return spread(kernel, "spread_token_grads", (part, *sets, *blocks), 1 + reps, blocks, kinds, 5)


def spread_heads(sets, blocks, after, wide):
    reps = len(blocks)

    def kernel(*refs):
        spread_heads_kernel(*refs, reps=reps, wide=wide)

    return spread(kernel, "spread_head_grads", (*sets, *blocks, after), reps, blocks, [(RANK, wide)] * 6, 4, rest=1)


def body(
    hidden,
    out_grad,
    clip_lengths,
    adapter_index,
    w_query,
    w_key,
    w_value,
    w_output,
    w_up,
    w_down,
    a_query,
    b_query,
    a_key,
    b_key,
    a_value,
    b_value,
    a_output,
    b_output,
    a_up,
    b_up,
    a_down,
    b_down,
):
    shards = lax.axis_size("shard")
    reps = lax.axis_size("rep")
    wide = D // shards
    shard = lax.axis_index("shard")
    rep = lax.axis_index("rep")
    part = rep % GROUP

    def mate(value, flip):
        return lax.ppermute(value, "rep", [(i, i ^ flip) for i in range(reps)])

    def across(value):
        return lax.all_to_all(value, "shard", split_axis=0, concat_axis=0, tiled=True)

    def turned(table):
        return jnp.transpose(table, (0, 2, 1))

    def group_gather(value):
        other = mate(value, 2)
        return [value, mate(value, 1), other, mate(other, 1)]

    place = jnp.where(shard % 2 == 0, shard // 2, shards - 1 - shard // 2)
    meta = jnp.stack([shard, part, clip_lengths[0], rep & 1, place]).astype(jnp.int32)
    part_only = part[None].astype(jnp.int32)
    sets = [adapter_index] + [mate(adapter_index, flip) for flip in range(1, reps)]
    enters = [turned(t) for t in (a_query, a_key, a_value)]
    leaves = [b_query, b_key, b_value]

    narrow = enters + [turned(a_output), turned(a_up), b_output, b_down]
    bundle = pack_first(adapter_index, meta, hidden, w_output, narrow)
    cols, halves = pack_columns(meta, (w_query, w_key, w_value), bundle, shards)
    feed, down_own = pack_feed(sets[:GROUP], part_only, w_up, w_down, leaves, turned(a_down), b_up, bundle, shards)
    cols = across(cols)
    held = {}

    def between(k, arrivals):
        if k == 1:
            return lax.optimization_barrier((*arrivals, halves, feed))[:2]
        if k == 2:
            below, above, held["cols"] = lax.optimization_barrier((*arrivals, cols))
            return below, above
        if k == shards // 2 - 1:
            below, above, held["feed"], held["down"] = lax.optimization_barrier((*arrivals, feed, down_own))
            return below, above
        return lax.optimization_barrier(arrivals)

    pieces = ring_pieces(bundle, shards, between)
    cols = held["cols"]
    cols_mate = mate(cols, 1)
    ff_moved = lax.all_gather(held["feed"], "shard", axis=0, tiled=True)
    grads_out = group_gather(out_grad)

    first, qkv, inner_qkv, adapters, out_quarter = project_qkv(meta, adapter_index, cols, cols_mate, pieces, leaves)
    stage = {}

    def down_between(k, arrivals):
        if k == 1:
            below, above, stage["qkv"] = lax.optimization_barrier((*arrivals, qkv))
            stage["out_weights"] = group_gather(out_quarter)
            packed, stage["ctx"], stage["lse"] = attend(stage["qkv"], shards)
            stage["packed"] = packed
            return below, above
        if k == 2:
            below, above, packed = lax.optimization_barrier((*arrivals, stage["packed"]))
            stage["moved"] = across(packed)
            return below, above
        if k == 3:
            below, above, stage["moved"], stage["ff"] = lax.optimization_barrier((*arrivals, stage["moved"], ff_moved))
            return below, above
        return lax.optimization_barrier(arrivals)

    down_pieces = ring_pieces(held["down"], shards, down_between)
    ff_all = stage["ff"]
    qkv, ctx, lse, out_weights = stage["qkv"], stage["ctx"], stage["lse"], stage["out_weights"]
    context, middle, cat, inner_o = project_output(
        meta, stage["moved"], out_weights, adapters, hidden, out_grad
    )
    halves, lse = lax.optimization_barrier((halves, lse))
    qkv_quarter = lax.all_gather(halves, "shard", axis=0, tiled=True)

    grad_act, down_weight = down_back(meta, down_pieces, grads_out)
    other = mate(cat, 2)
    other, grad_act = lax.optimization_barrier((other, grad_act))
    cats = [cat, mate(cat, 1), other, mate(other, 1)]
    act, pre, keep, give = up_both(ff_all, grad_act, cats)

    def near_sum(keep, give):
        near = mate(give, 1)
        return near, (keep[1].astype(F32) + near[1].astype(F32)).astype(BF)

    near, far = near_sum(keep, give)
    far = mate(far, 2)
    keep_d, give_d, pieces_d = down_forward(down_weight, ff_all, act, pre, cats)
    give_d, far = lax.optimization_barrier((give_d, far))
    near_d, far_d = near_sum(keep_d, give_d)
    far_d = mate(far_d, 2)
    grad_middle, dctx, attn, gi_up, gi_o = middle_back(
        meta, keep, near, far, middle, out_grad, out_weights, adapters, shards
    )
    dctx_moved = across(dctx)
    layer_out, token_pieces = token_grads(
        meta, keep_d, near_d, far_d, middle, out_grad, adapters, cat, gi_up, context, gi_o, attn, inner_o, pieces_d,
        shards=shards,
    )
    early = across(token_pieces)
    qkv_quarter, token_pieces = lax.optimization_barrier((qkv_quarter, token_pieces))
    qkv_weights = group_gather(qkv_quarter)
    lse_rows = lse.reshape(lse.shape[0], 1, lse.shape[1])
    dqkv, head_out = attend_back(
        adapter_index, qkv, dctx_moved, ctx, lse_rows, first, inner_qkv, leaves, token_pieces, shards
    )
    dqkv, early = lax.optimization_barrier((dqkv, early))
    dqkv_moved = across(dqkv)

    def over_reps(value):
        return [value] + [mate(value, flip) for flip in range(1, reps)]

    early = jnp.sum(early.astype(F32), axis=0).astype(BF)
    token_outs = spread_tokens(part_only, sets, over_reps(early), wide)
    summed = sum_pieces(dqkv_moved, head_out)
    input_grad = input_back(
        meta, dqkv_moved, qkv_weights, adapters, ff_all, hidden, grad_middle, token_outs[1], shards
    )
    outs = spread_heads(sets, over_reps(summed), input_grad, wide) + token_outs
    return (layer_out, input_grad, *outs)


def solution(mesh):
    rows = P("shard", None)
    enter = P(None, "shard", None)
    leave = P(None, None, "shard")
    tokens = P(("rep", "shard"), None)
    return jax.shard_map(
        body,
        mesh=mesh,
        in_specs=(tokens, tokens, P("rep"), P("rep")) + (rows,) * 6 + (enter, leave) * 6,
        out_specs=(tokens, tokens) + (enter, leave) * 6,
        check_vma=False,
    )
```

time: 604 us -> 395 us (0.65); the launches traced: 594 us -> 393 us
  blocking collectives: 198 us -> 0 us
  Pallas kernels: 27.9 us -> 139 us
  local copies, waits for them, and re-layouts: 122 us -> 15.5 us
  matrix products: 81.4 us -> 0 us
  waiting for transfers between devices: 76.9 us -> 146 us
  starting transfers between devices: 39.3 us -> 72.6 us
  other arithmetic: 26.1 us -> 3.67 us
  between operations: 22.4 us -> 16.2 us
    all_gather x5 -> x0, blocking collectives: 194 us -> none  [the longest x1 76.2 us: body(): enters = lax.all_gather(enter_pack, 'shard', axis=0, tiled=True)]
    pallas_call x2 -> x16, Pallas kernels: 27.9 us -> 139 us  [the longest x12 91.6 us: call(): pl.pallas_call(kernel, out_shape=outs, in_specs=specs, out_specs=[VMEM] *...]
    dot_general x64 -> x0, matrix products: 81.4 us -> none  [the longest x18 35.9 us: dot(): return jnp.dot(left, right, preferred_element_type=F32)]
    ppermute x0 -> x16, waiting for transfers between devices: none -> 61.8 us  [the longest x6 31.2 us: ring_pieces(): below = lax.ppermute(below, 'shard', onward)]
    all_to_all x5, waiting for transfers between devices: 49.5 us -> 15.2 us  [across(): lax.all_to_all(value, 'shard', split_axis=0, concat_axis=0, tiled=True)]
    ppermute x0 -> x16, starting transfers between devices: none -> 32.1 us  [the longest x2 12.6 us: ring_pieces(): pieces.append((lax.ppermute(above[half:], 'shard', back), far, half))]
    reshape x24 -> x1, local copies, waits for them, and re-layouts: 27.8 us -> 0.62 us  [body(): lse_rows = lse.reshape(lse.shape[0], 1, lse.shape[1])]
    ppermute x27 -> x26, waiting for transfers between devices: 25.9 us -> 49.2 us  [mate(): return lax.ppermute(value, 'rep', [(i, i ^ flip) for i in range(reps)])]
  transfers between devices with their start and end apart: 37 -> 49, of which waited for: 8 -> 26; matrix products, arithmetic and copies ran while one was open for 36% -> 3% of each run, Pallas kernels for 5% -> 29%
where the time goes in v2:
time: 395 us; the launch traced here: 393 us
  waiting for transfers between devices  146 us (37%)
  Pallas kernels  139 us (35%)
  starting transfers between devices  72.6 us (18%)
  between operations  16.2 us (4%)
  local copies, waits for them, and re-layouts  15.5 us (4%)
    pallas_call x12, Pallas kernels, call(): pl.pallas_call(kernel, out_shape=outs, in_specs=specs, out_specs=[VMEM] *...  91.6 us
    ppermute x26, waiting for transfers between devices, mate(): return lax.ppermute(value, 'rep', [(i, i ^ flip) for i in range(reps)])  49.2 us
    ppermute x6, waiting for transfers between devices, ring_pieces(): below = lax.ppermute(below, 'shard', onward)  31.2 us
    pallas_call x1, Pallas kernels, attend_back(): pl.pallas_call(kernel, out_shape=outs, grid_spec=pltpu.PrefetchScalarGrid...  24.9 us
    all_to_all x5, starting transfers between devices, across(): lax.all_to_all(value, 'shard', split_axis=0, concat_axis=0, tiled=True)  23.7 us
    ppermute x6, waiting for transfers between devices, ring_pieces(): above = lax.ppermute(above, 'shard', back)  20.3 us
    all_gather x1, waiting for transfers between devices, body(): qkv_quarter = lax.all_gather(halves, 'shard', axis=0, tiled=True)  19.4 us
    ppermute x26, starting transfers between devices, mate(): return lax.ppermute(value, 'rep', [(i, i ^ flip) for i in range(reps)])  16.7 us
  transfers between devices with their start and end apart: 49, of which 26 were waited for; matrix products, arithmetic and copies ran while one was open for 3% of the time, Pallas kernels for 29%

profile of v2, /device:TPU:0, one launch (start us, length us, event | category | flops | bytes accessed | tf_op | source)
XLA Modules:
  0.0 392.8 jit_solution(7086867349447149486)
XLA Ops:
  19.8 6.0 %all-to-all-start = ((bf16[8,160,256]{2,1,0:T(8,128)(2,1)}), bf16[8,160,256]{2,1,0:T(8,128)(2,1)S(1)}, u32[]{:S(2)}, u32[]{:S(2)}) async-start(bf16[8,160,256]{2,1,0:T(8,128)(2,1)} %get-tuple-element.93), calls=%async_computation | async-start | bytes 1310720 | tf_op jit(solution)/shard_map/all_to_all | solution.py:932
  25.9 5.4 %pack_feed.1 = (bf16[160,1536]{1,0:T(8,128)(2,1)}, bf16[160,1280]{1,0:T(8,128)(2,1)}) custom-call(s32[1]{0:T(128)S(6)} %copy.47.chosen.refs_0_.refs_1_, s32[1]{0:T(128)} %collective-permute-done.2.refs_1_.refs_2_, s32[1]{0:T(128)} %collective-permute-done.3.refs_2_.refs_3_, s32[1]{0:T(128)} %collective-permute-done.4.refs_3_.refs_4_, ...), custom_call_target="tpu_custom_call" | custom-call | flops 5750000128 | tf_op jit(solution)/shard_map/pack_feed/pallas_call | solution.py:216
  35.2 13.0 %all-to-all-done.refs_1_ = bf16[8,160,256]{2,1,0:T(8,128)(2,1)S(1)} async-done(((bf16[8,160,256]{2,1,0:T(8,128)(2,1)}), bf16[8,160,256]{2,1,0:T(8,128)(2,1)S(1)}, u32[]{:S(2)}, u32[]{:S(2)}) %all-to-all-start) | async-done | bytes 655392 | tf_op jit(solution)/shard_map/all_to_all | solution.py:932
  48.2 6.7 %collective-permute-done.5.refs_6_ = bf16[192,1792]{1,0:T(8,128)(2,1)} collective-permute-done((bf16[192,1792]{1,0:T(8,128)(2,1)S(1)}, bf16[192,1792]{1,0:T(8,128)(2,1)}, u32[]{:S(2)}, u32[]{:S(2)}) %collective-permute-start.5) | collective-permute-done | bytes 688160 | tf_op jit(solution)/shard_map/ppermute | solution.py:243
  62.3 13.9 %collective-permute-done.7.refs_8_ = bf16[192,1792]{1,0:T(8,128)(2,1)S(1)} collective-permute-done((bf16[192,1792]{1,0:T(8,128)(2,1)}, bf16[192,1792]{1,0:T(8,128)(2,1)S(1)}, u32[]{:S(2)}, u32[]{:S(2)}) %collective-permute-start.7) | collective-permute-done | bytes 688160 | tf_op jit(solution)/shard_map/ppermute | solution.py:243
  82.6 7.7 %collective-permute-done.12.refs_10_ = bf16[96,1792]{1,0:T(8,128)(2,1)S(1)} collective-permute-done((bf16[96,1792]{1,0:T(8,128)(2,1)S(1)}, bf16[96,1792]{1,0:T(8,128)(2,1)S(1)}, u32[]{:S(2)}, u32[]{:S(2)}) %collective-permute-start.12) | collective-permute-done | bytes 344096 | tf_op jit(solution)/shard_map/ppermute | solution.py:248
  93.6 14.9 %project_qkv.1 = (bf16[1536,1280]{1,0:T(8,128)(2,1)}, bf16[1536,768]{1,0:T(8,128)(2,1)}, bf16[1536,48]{1,0:T(8,128)(2,1)}, bf16[1280,128]{1,0:T(8,128)(2,1)}, bf16[1280,320]{1,0:T(8,128)(2,1)}) custom-call(s32[1]{0:T(128)S(6)} %copy.47.chosen.refs_0_.refs_1_, s32[5]{0:T(128)} %stack.19.meta.refs_0_, bf16[8,160,256]{2,1,0:T(8,128)(2,1)} %copy-done.2, ...), custom_call_target="tpu_custom_call" | custom-call | flops 16099999744 | tf_op jit(solution)/shard_map/project_qkv/pallas_call | solution.py:334
  116.1 12.8 %attention_forward.1 = (bf16[8,48,640]{2,1,0:T(8,128)(2,1)}, bf16[1536,256]{1,0:T(8,128)(2,1)}, f32[2,1536,1]{2,1,0:T(8,128)}) custom-call(bf16[1536,768]{1,0:T(8,128)(2,1)} %get-tuple-element.104.refs_0_), custom_call_target="tpu_custom_call" | custom-call | flops 13799999488 | tf_op jit(solution)/shard_map/attention_forward/pallas_call | solution.py:83
  130.9 9.7 %collective-permute-done.15.refs_4_ = bf16[160,1280]{1,0:T(8,128)(2,1)} collective-permute-done((bf16[160,1280]{1,0:T(8,128)(2,1)}, bf16[160,1280]{1,0:T(8,128)(2,1)}, u32[]{:S(2)}, u32[]{:S(2)}) %collective-permute-start.15) | collective-permute-done | bytes 409632 | tf_op jit(solution)/shard_map/ppermute | solution.py:244
  150.3 8.6 %collective-permute-done.21.refs_11_ = bf16[192,1280]{1,0:T(8,128)(2,1)} collective-permute-done((bf16[192,1280]{1,0:T(8,128)(2,1)}, bf16[192,1280]{1,0:T(8,128)(2,1)}, u32[]{:S(2)}, u32[]{:S(2)}) %collective-permute-start.21) | collective-permute-done | bytes 491552 | tf_op jit(solution)/shard_map/ppermute | solution.py:929
  162.0 8.6 %collective-permute-done.16.refs_5_ = bf16[160,1280]{1,0:T(8,128)(2,1)} collective-permute-done((bf16[160,1280]{1,0:T(8,128)(2,1)}, bf16[160,1280]{1,0:T(8,128)(2,1)}, u32[]{:S(2)}, u32[]{:S(2)}) %collective-permute-start.16) | collective-permute-done | bytes 409632 | tf_op jit(solution)/shard_map/ppermute | solution.py:243
  177.2 11.1 %collective-permute-start.19 = (bf16[80,1280]{1,0:T(8,128)(2,1)S(1)}, bf16[80,1280]{1,0:T(8,128)(2,1)S(1)}, u32[]{:S(2)}, u32[]{:S(2)}) collective-permute-start(bf16[80,1280]{1,0:T(8,128)(2,1)S(1)} %slice.27), channel_id=1, source_target_pairs={{2,0},{4,2},{6,4},{7,6},{5,7},{3,5},{1,3},{0,1},{10,8},{12,10},{14... | collective-permute-start | bytes 614408 | tf_op jit(solution)/shard_map/ppermute | solution.py:249
  188.4 5.9 %project_output.1 = (bf16[192,1280]{1,0:T(8,128)(2,1)}, f32[192,1280]{1,0:T(8,128)}, bf16[192,1408]{1,0:T(8,128)(2,1)}, bf16[192,16]{1,0:T(8,128)(2,1)}) custom-call(s32[5]{0:T(128)} %stack.19.meta.refs_0_, bf16[8,48,640]{2,1,0:T(8,128)(2,1)} %all-to-all-done.1.moved, bf16[1280,320]{1,0:T(8,128)(2,1)} %get-tuple-element.115.w0, bf16[1280,320]{1,0:T(8,128)(2,1)} %copy.39.w1, ...), custom_call_target="tpu_custom_call" | custom-call | flops 6899999744 | tf_op jit(solution)/shard_map/project_output/pallas_call | solution.py:83
  197.4 8.1 %down_backward.1 = (f32[768,1280]{1,0:T(8,128)}, bf16[8,160,1280]{2,1,0:T(8,128)(2,1)}) custom-call(s32[5]{0:T(128)} %stack.19.meta.refs_0_, bf16[160,1280]{1,0:T(8,128)(2,1)} %get-tuple-element.97.refs_0_, bf16[160,1280]{1,0:T(8,128)(2,1)} %collective-permute-done.9.refs_1_, bf16[160,1280]{1,0:T(8,128)(2,1)} %collective-permute-done.10.refs_2_, ...), custom_call_target="tpu_custom_call" | custom-call | flops 8049999872 | tf_op jit(solution)/shard_map/down_backward/pallas_call | solution.py:83
  209.5 15.5 %up_forward_backward.1 = (bf16[768,1280]{1,0:T(8,128)(2,1)}, bf16[768,1280]{1,0:T(8,128)(2,1)}, bf16[2,192,1408]{2,1,0:T(8,128)(2,1)}, bf16[2,192,1408]{2,1,0:T(8,128)(2,1)}) custom-call(bf16[1280,1536]{1,0:T(8,128)(2,1)} %all-gather.3.cloned.1.call-done.w_ref.adapters.refs_7_, f32[768,1280]{1,0:T(8,128)} %get-tuple-element.119.grad_ref, ...), custom_call_target="tpu_custom_call" | custom-call | flops 17250000896 | tf_op jit(solution)/shard_map/up_forward_backward/pallas_call | solution.py:83
  231.0 8.4 %down_forward.1 = (bf16[2,192,1408]{2,1,0:T(8,128)(2,1)}, bf16[2,192,1408]{2,1,0:T(8,128)(2,1)}, bf16[128,1280]{1,0:T(8,128)(2,1)}) custom-call(bf16[8,160,1280]{2,1,0:T(8,128)(2,1)} %get-tuple-element.112.w_ref, bf16[768,1280]{1,0:T(8,128)(2,1)} %get-tuple-element.121.act_ref, bf16[768,1280]{1,0:T(8,128)(2,1)} %get-tuple-element.122.pre_ref, ...), custom_call_target="tpu_custom_call" | custom-call | flops 10350000128 | tf_op jit(solution)/shard_map/down_forward/pallas_call | solution.py:83
  249.9 7.8 %middle_backward.1 = (f32[192,1280]{1,0:T(8,128)}, bf16[8,48,640]{2,1,0:T(8,128)(2,1)}, bf16[192,1280]{1,0:T(8,128)(2,1)}, bf16[192,16]{1,0:T(8,128)(2,1)}, bf16[192,16]{1,0:T(8,128)(2,1)}) custom-call(s32[5]{0:T(128)} %stack.19.meta.refs_0_, bf16[2,192,1408]{2,1,0:T(8,128)(2,1)} %get-tuple-element.125.keep, bf16[2,192,1408]{2,1,0:T(8,128)(2,1)} %copy-done.4, ...), custom_call_target="tpu_custom_call" | custom-call | flops 8049999872 | tf_op jit(solution)/shard_map/middle_backward/pallas_call | solution.py:83
  268.0 19.4 %all-gather.5.cloned.1.call-done.refs_2_ = bf16[1280,1024]{1,0:T(8,128)(2,1)} async-done(((bf16[160,1024]{1,0:T(8,128)(2,1)}), bf16[1280,1024]{1,0:T(8,128)(2,1)}) %all-gather.5.cloned.1.call-update) | async-done | bytes 2621456 | tf_op jit(solution)/shard_map/all_gather | solution.py:998
  292.5 24.9 %attention_backward.1 = (bf16[8,208,512]{2,1,0:T(8,128)(2,1)}, bf16[16,512]{1,0:T(8,128)(2,1)}) custom-call(s32[1]{0:T(128)S(6)} %copy.47.chosen.refs_0_.refs_1_, bf16[1536,768]{1,0:T(8,128)(2,1)} %get-tuple-element.104.refs_0_, bf16[8,48,640]{2,1,0:T(8,128)(2,1)} %copy-done.3, bf16[1536,256]{1,0:T(8,128)(2,1)} %get-tuple-element.138.refs_2_, ...), custom_call_target="tpu_custom_call" | custom-call | flops 27599998976 | tf_op jit(solution)/shard_map/attention_backward/pallas_call | solution.py:496
  317.4 6.3 %all-to-all-start.4 = ((bf16[8,208,512]{2,1,0:T(8,128)(2,1)}), bf16[8,208,512]{2,1,0:T(8,128)(2,1)S(1)}, u32[]{:S(2)}, u32[]{:S(2)}) async-start(bf16[8,208,512]{2,1,0:T(8,128)(2,1)} %get-tuple-element.147), calls=%async_computation.4 | async-start | bytes 3407872 | tf_op jit(solution)/shard_map/all_to_all | solution.py:932
  323.7 22.8 %collective-permute-done.34.refs_4_ = bf16[1280,1024]{1,0:T(8,128)(2,1)} collective-permute-done((bf16[1280,1024]{1,0:T(8,128)(2,1)}, bf16[1280,1024]{1,0:T(8,128)(2,1)}, u32[]{:S(2)}, u32[]{:S(2)}) %collective-permute-start.34) | collective-permute-done | bytes 2621472 | tf_op jit(solution)/shard_map/ppermute | solution.py:929
  353.5 7.1 %spread_token_grads.1 = (f32[8,16,160]{2,1,0:T(8,128)}, f32[8,16,160]{2,1,0:T(8,128)}, f32[8,16,160]{2,1,0:T(8,128)}, f32[8,16,640]{2,1,0:T(8,128)}, f32[8,16,640]{2,1,0:T(8,128)}, /*index=5*/f32[8,16,160]{2,1,0:T(8,128)}) custom-call(s32[1]{0:T(128)} %bitcast.1.refs_4_.refs_0_, s32[1]{0:T(128)S(6)} %copy.47.chosen.refs_0_.refs_1_, ...), custom_call_target="tpu_custom_call" | custom-call | flops 5750000128 | tf_op jit(solution)/shard_map/spread_token_grads/pallas_call | solution.py:83
  368.0 10.6 %input_backward.1.refs_8_ = bf16[192,1280]{1,0:T(8,128)(2,1)} custom-call(s32[5]{0:T(128)} %stack.19.meta.refs_0_, bf16[8,208,512]{2,1,0:T(8,128)(2,1)} %copy-done, bf16[1280,1024]{1,0:T(8,128)(2,1)} %all-gather.5.cloned.1.call-done.refs_2_, bf16[1280,1024]{1,0:T(8,128)(2,1)} %collective-permute-done.33.refs_3_, ...), custom_call_target="tpu_custom_call" | custom-call | flops 11500000256 | tf_op jit(solution)/shard_map/input_backward/pallas_call | solution.py:83
  379.8 5.7 %spread_head_grads.1 = (f32[8,16,160]{2,1,0:T(8,128)}, f32[8,16,160]{2,1,0:T(8,128)}, f32[8,16,160]{2,1,0:T(8,128)}, f32[8,16,160]{2,1,0:T(8,128)}, f32[8,16,160]{2,1,0:T(8,128)}, /*index=5*/f32[8,16,160]{2,1,0:T(8,128)}) custom-call(s32[1]{0:T(128)S(6)} %copy.47.chosen.refs_0_.refs_1_, s32[1]{0:T(128)} %collective-permute-done.2.refs_1_.refs_2_, ...), custom_call_target="tpu_custom_call" | custom-call | flops 4600000000 | tf_op jit(solution)/shard_map/spread_head_grads/pallas_call | solution.py:83
  (162 shorter events, 115.7 us)
Async XLA Ops:
  11.6 19.8 %collective-permute-start = (bf16[192,1792]{1,0:T(8,128)(2,1)}, bf16[192,1792]{1,0:T(8,128)(2,1)S(1)}, u32[]{:S(2)}, u32[]{:S(2)}) collective-permute-start(bf16[192,1792]{1,0:T(8,128)(2,1)} %pack_first.1.after.refs_18_.refs_3_), channel_id=1, source_target_pairs={{0,2},{2,4},{4,6},{6,7},{7,5},{5,3},{3,1},{1,0},{8,10},{10,12},{12... | collective-permute-start | bytes 2064392 | tf_op jit(solution)/shard_map/ppermute | solution.py:243
  19.8 28.4 %all-to-all-start = ((bf16[8,160,256]{2,1,0:T(8,128)(2,1)}), bf16[8,160,256]{2,1,0:T(8,128)(2,1)S(1)}, u32[]{:S(2)}, u32[]{:S(2)}) async-start(bf16[8,160,256]{2,1,0:T(8,128)(2,1)} %get-tuple-element.93), calls=%async_computation | async-start | bytes 1310720 | tf_op jit(solution)/shard_map/all_to_all | solution.py:932
  25.8 146.9 %all-gather.3.cloned.1.call-start = ((), (), s32[]{:S(2)}) async-start(), calls=%async_computation.5 | async-start | bytes 4423680 | tf_op jit(solution)/shard_map/all_gather | solution.py:969
  33.2 21.7 %collective-permute-start.5 = (bf16[192,1792]{1,0:T(8,128)(2,1)S(1)}, bf16[192,1792]{1,0:T(8,128)(2,1)}, u32[]{:S(2)}, u32[]{:S(2)}) collective-permute-start(bf16[192,1792]{1,0:T(8,128)(2,1)S(1)} %collective-permute-done.refs_4_), channel_id=1, source_target_pairs={{0,2},{2,4},{4,6},{6,7},{7,5},{5,3},{3,1},{1,0},{8,10},{10,12},{12... | collective-permute-start | bytes 2064392 | tf_op jit(solution)/shard_map/ppermute | solution.py:243
  34.7 22.5 %collective-permute-start.6 = (bf16[192,1792]{1,0:T(8,128)(2,1)S(1)}, bf16[192,1792]{1,0:T(8,128)(2,1)}, u32[]{:S(2)}, u32[]{:S(2)}) collective-permute-start(bf16[192,1792]{1,0:T(8,128)(2,1)S(1)} %collective-permute-done.1.refs_5_), channel_id=1, source_target_pairs={{2,0},{4,2},{6,4},{7,6},{5,7},{3,5},{1,3},{0,1},{10,8},{12,10},{14... | collective-permute-start | bytes 2064392 | tf_op jit(solution)/shard_map/ppermute | solution.py:244
  57.2 19.0 %collective-permute-start.7 = (bf16[192,1792]{1,0:T(8,128)(2,1)}, bf16[192,1792]{1,0:T(8,128)(2,1)S(1)}, u32[]{:S(2)}, u32[]{:S(2)}) collective-permute-start(bf16[192,1792]{1,0:T(8,128)(2,1)} %collective-permute-done.5.refs_6_), channel_id=1, source_target_pairs={{0,2},{2,4},{4,6},{6,7},{7,5},{5,3},{3,1},{1,0},{8,10},{10,12},{12... | collective-permute-start | bytes 2064392 | tf_op jit(solution)/shard_map/ppermute | solution.py:243
  80.6 31.2 %collective-permute-start.9 = (bf16[160,1280]{1,0:T(8,128)(2,1)}, bf16[160,1280]{1,0:T(8,128)(2,1)}, u32[]{:S(2)}, u32[]{:S(2)}) collective-permute-start(bf16[160,1280]{1,0:T(8,128)(2,1)} %get-tuple-element.97.refs_0_), channel_id=1, source_target_pairs={{0,2},{2,4},{4,6},{6,7},{7,5},{5,3},{3,1},{1,0},{8,10},{10,12},{12... | collective-permute-start | bytes 1228808 | tf_op jit(solution)/shard_map/ppermute | solution.py:243
  81.3 32.8 %collective-permute-start.10 = (bf16[160,1280]{1,0:T(8,128)(2,1)}, bf16[160,1280]{1,0:T(8,128)(2,1)}, u32[]{:S(2)}, u32[]{:S(2)}) collective-permute-start(bf16[160,1280]{1,0:T(8,128)(2,1)} %get-tuple-element.97.refs_0_), channel_id=1, source_target_pairs={{2,0},{4,2},{6,4},{7,6},{5,7},{3,5},{1,3},{0,1},{10,8},{12,10},{14... | collective-permute-start | bytes 1228808 | tf_op jit(solution)/shard_map/ppermute | solution.py:244
  110.0 34.8 %collective-permute-start.24 = (bf16[1280,320]{0,1:T(8,128)(2,1)S(1)}, bf16[1280,320]{0,1:T(8,128)(2,1)S(1)}, u32[]{:S(2)}, u32[]{:S(2)}) collective-permute-start(bf16[1280,320]{0,1:T(8,128)(2,1)S(1)} %copy.37), channel_id=1, source_target_pairs={{0,16},{8,24},{16,0},{24,8},{1,17},{9,25},{17,1},{25,9},{2,18},{10... | collective-permute-start | bytes 2457608 | tf_op jit(solution)/shard_map/ppermute | solution.py:929
  114.1 26.5 %collective-permute-start.15 = (bf16[160,1280]{1,0:T(8,128)(2,1)}, bf16[160,1280]{1,0:T(8,128)(2,1)}, u32[]{:S(2)}, u32[]{:S(2)}) collective-permute-start(bf16[160,1280]{1,0:T(8,128)(2,1)} %collective-permute-done.10.refs_2_), channel_id=1, source_target_pairs={{2,0},{4,2},{6,4},{7,6},{5,7},{3,5},{1,3},{0,1},{10,8},{12,10},{14... | collective-permute-start | bytes 1228808 | tf_op jit(solution)/shard_map/ppermute | solution.py:244
  140.6 32.1 %all-to-all-start.1 = ((bf16[8,48,640]{2,1,0:T(8,128)(2,1)}), bf16[8,48,640]{2,1,0:T(8,128)(2,1)}, u32[]{:S(2)}, u32[]{:S(2)}) async-start(bf16[8,48,640]{2,1,0:T(8,128)(2,1)} %get-tuple-element.108), calls=%async_computation.1 | async-start | bytes 983040 | tf_op jit(solution)/shard_map/all_to_all | solution.py:932
  144.7 142.7 %all-gather.5.cloned.1.call-start = ((), (), s32[]{:S(2)}) async-start(), calls=%async_computation.6 | async-start | bytes 2949120 | tf_op jit(solution)/shard_map/all_gather | solution.py:998
  147.0 23.6 %collective-permute-start.16 = (bf16[160,1280]{1,0:T(8,128)(2,1)}, bf16[160,1280]{1,0:T(8,128)(2,1)}, u32[]{:S(2)}, u32[]{:S(2)}) collective-permute-start(bf16[160,1280]{1,0:T(8,128)(2,1)} %collective-permute-done.14.refs_3_), channel_id=1, source_target_pairs={{0,2},{2,4},{4,6},{6,7},{7,5},{5,3},{3,1},{1,0},{8,10},{10,12},{12... | collective-permute-start | bytes 1228808 | tf_op jit(solution)/shard_map/ppermute | solution.py:243
  148.7 24.0 %collective-permute-start.17 = (bf16[160,1280]{1,0:T(8,128)(2,1)}, bf16[160,1280]{1,0:T(8,128)(2,1)}, u32[]{:S(2)}, u32[]{:S(2)}) collective-permute-start(bf16[160,1280]{1,0:T(8,128)(2,1)} %collective-permute-done.15.refs_4_), channel_id=1, source_target_pairs={{2,0},{4,2},{6,4},{7,6},{5,7},{3,5},{1,3},{0,1},{10,8},{12,10},{14... | collective-permute-start | bytes 1228808 | tf_op jit(solution)/shard_map/ppermute | solution.py:244
  158.9 37.0 %collective-permute-start.20 = (bf16[192,1280]{1,0:T(8,128)(2,1)}, bf16[192,1280]{1,0:T(8,128)(2,1)}, u32[]{:S(2)}, u32[]{:S(2)}) collective-permute-start(bf16[192,1280]{1,0:T(8,128)(2,1)} %out_grad.5), channel_id=1, source_target_pairs={{0,8},{8,0},{16,24},{24,16},{1,9},{9,1},{17,25},{25,17},{2,10},{10... | collective-permute-start | bytes 1474568 | tf_op jit(solution)/shard_map/ppermute | solution.py:929
  158.9 37.0 %collective-permute-start.22 = (bf16[192,1280]{1,0:T(8,128)(2,1)}, bf16[192,1280]{1,0:T(8,128)(2,1)S(1)}, u32[]{:S(2)}, u32[]{:S(2)}) collective-permute-start(bf16[192,1280]{1,0:T(8,128)(2,1)} %collective-permute-done.21.refs_11_), channel_id=1, source_target_pairs={{0,8},{8,0},{16,24},{24,16},{1,9},{9,1},{17,25},{25,17},{2,10},{10... | collective-permute-start | bytes 1474568 | tf_op jit(solution)/shard_map/ppermute | solution.py:929
  173.7 22.2 %collective-permute-start.18 = (bf16[80,1280]{1,0:T(8,128)(2,1)S(1)}, bf16[80,1280]{1,0:T(8,128)(2,1)S(1)}, u32[]{:S(2)}, u32[]{:S(2)}) collective-permute-start(bf16[80,1280]{1,0:T(8,128)(2,1)S(1)} %slice.26), channel_id=1, source_target_pairs={{0,2},{2,4},{4,6},{6,7},{7,5},{5,3},{3,1},{1,0},{8,10},{10,12},{12... | collective-permute-start | bytes 614408 | tf_op jit(solution)/shard_map/ppermute | solution.py:248
  177.2 18.7 %collective-permute-start.19 = (bf16[80,1280]{1,0:T(8,128)(2,1)S(1)}, bf16[80,1280]{1,0:T(8,128)(2,1)S(1)}, u32[]{:S(2)}, u32[]{:S(2)}) collective-permute-start(bf16[80,1280]{1,0:T(8,128)(2,1)S(1)} %slice.27), channel_id=1, source_target_pairs={{2,0},{4,2},{6,4},{7,6},{5,7},{3,5},{1,3},{0,1},{10,8},{12,10},{14... | collective-permute-start | bytes 614408 | tf_op jit(solution)/shard_map/ppermute | solution.py:249
  257.6 31.3 %all-to-all-start.2 = ((bf16[8,48,640]{2,1,0:T(8,128)(2,1)}), bf16[8,48,640]{2,1,0:T(8,128)(2,1)S(1)}, u32[]{:S(2)}, u32[]{:S(2)}) async-start(bf16[8,48,640]{2,1,0:T(8,128)(2,1)} %get-tuple-element.137), calls=%async_computation.2 | async-start | bytes 983040 | tf_op jit(solution)/shard_map/all_to_all | solution.py:932
  287.4 59.1 %collective-permute-start.34 = (bf16[1280,1024]{1,0:T(8,128)(2,1)}, bf16[1280,1024]{1,0:T(8,128)(2,1)}, u32[]{:S(2)}, u32[]{:S(2)}) collective-permute-start(bf16[1280,1024]{1,0:T(8,128)(2,1)} %all-gather.5.cloned.1.call-done.refs_2_), channel_id=1, source_target_pairs={{0,16},{8,24},{16,0},{24,8},{1,17},{9,25},{17,1},{25,9},{2,18},{10... | collective-permute-start | bytes 7864328 | tf_op jit(solution)/shard_map/ppermute | solution.py:929
  288.9 28.5 %all-to-all-start.3 = ((bf16[8,64,512]{2,1,0:T(8,128)(2,1)}), bf16[8,64,512]{2,1,0:T(8,128)(2,1)S(1)}, u32[]{:S(2)}, u32[]{:S(2)}) async-start(bf16[8,64,512]{2,1,0:T(8,128)(2,1)} %get-tuple-element.145.refs_9_), calls=%async_computation.3 | async-start | bytes 1048576 | tf_op jit(solution)/shard_map/all_to_all | solution.py:932
  317.4 45.4 %all-to-all-start.4 = ((bf16[8,208,512]{2,1,0:T(8,128)(2,1)}), bf16[8,208,512]{2,1,0:T(8,128)(2,1)S(1)}, u32[]{:S(2)}, u32[]{:S(2)}) async-start(bf16[8,208,512]{2,1,0:T(8,128)(2,1)} %get-tuple-element.147), calls=%async_computation.4 | async-start | bytes 3407872 | tf_op jit(solution)/shard_map/all_to_all | solution.py:932
  323.7 44.3 %collective-permute-start.33 = (bf16[1280,1024]{1,0:T(8,128)(2,1)}, bf16[1280,1024]{1,0:T(8,128)(2,1)}, u32[]{:S(2)}, u32[]{:S(2)}) collective-permute-start(bf16[1280,1024]{1,0:T(8,128)(2,1)} %all-gather.5.cloned.1.call-done.refs_2_), channel_id=1, source_target_pairs={{0,8},{8,0},{16,24},{24,16},{1,9},{9,1},{17,25},{25,17},{2,10},{10... | collective-permute-start | bytes 7864328 | tf_op jit(solution)/shard_map/ppermute | solution.py:929
  346.6 21.4 %collective-permute-start.35 = (bf16[1280,1024]{1,0:T(8,128)(2,1)}, bf16[1280,1024]{1,0:T(8,128)(2,1)}, u32[]{:S(2)}, u32[]{:S(2)}) collective-permute-start(bf16[1280,1024]{1,0:T(8,128)(2,1)} %collective-permute-done.34.refs_4_), channel_id=1, source_target_pairs={{0,8},{8,0},{16,24},{24,16},{1,9},{9,1},{17,25},{25,17},{2,10},{10... | collective-permute-start | bytes 7864328 | tf_op jit(solution)/shard_map/ppermute | solution.py:929
  (53 other events, 533.5 us)
Sparse Core Ops, SparseCore 0:
  78.5 90.7 all-gather.2
  225.3 62.0 all-gather.4
